TPU v7x, 256 devices: a whole 4x4x8 slice. The times are simulated.
256 devices in a mesh: gx: 8 (over z), gy: 8 (over x, core), gz: 4 (over y).
Axes of the slice: x: 4, y: 4, z: 8, core: 2. Of those that a mesh axis runs over, the one named last changes fastest.
Arguments:
- velocity: float32 [3, 64, 128, 1024], P(None, 'gz', 'gx', 'gy'), may hold values from -20 to 20
- owner: int32 [262144, 1], P(('gx', 'gy', 'gz')), may hold values from 0 to 63; in each aligned block of 1024 rows (0 to 1023, 1024 to 2047, ...) at most 64 rows name the same one
- cell_x: int32 [262144], P(('gx', 'gy', 'gz')), may hold values from 0 to 14
- cell_y: int32 [262144], P(('gx', 'gy', 'gz')), may hold values from 0 to 126
- cell_z: int32 [262144], P(('gx', 'gy', 'gz')), may hold values from 0 to 14
- query_weights: float32 [3, 262144], P(None, ('gx', 'gy', 'gz')), may hold values from 0 to 1
Outputs:
- query_stress: float32 [6, 262144], P(None, ('gx', 'gy', 'gz'))
Inputs may be any that keep to these rules, and one draw needn't show every extreme that they name: Among the queries held by one device, at most 64 name the same owner, and in every draw some owner is named by exactly 64 of them. `cell_x`: the corner cell plus one stays in the same brick.
All inputs are finite; a program needn't handle non-finite values.
Results may differ from a plain program's by a relative error of at most 0.0003.
Values sent between devices are 32-bit elements; how exact they have to be, the bound alone decides.
A program may use at most 64 MiB of HBM per device.

v0:
```python
import jax
import jax.numpy as jnp
from jax import lax
from jax.sharding import PartitionSpec as P

FW = 32


PAIRS = ((0, 0), (0, 1), (0, 2), (1, 1), (1, 2), (2, 2))


def padded(x, sides, width):
    for axis, dim in sides:
        devices, length = (lax.axis_size(axis), x.shape[dim])
        up = [(i, (i + 1) % devices) for i in range(devices)]
        down = [(j, i) for i, j in up]
        last = lax.slice_in_dim(x, length - width, length, axis=dim)
        initial = lax.slice_in_dim(x, 0, width, axis=dim)
        before = lax.ppermute(last, axis, up)
        after = lax.ppermute(initial, axis, down)
        x = jnp.concatenate([before, x, after], axis=dim)
    return x


def taps(radius, width):
    offsets = jnp.arange(2 * radius + 1).astype(jnp.float32) - radius
    values = jnp.exp(-6.0 * offsets * offsets / (width * width))
    return values / jnp.sum(values)


def band(length, radius, width):
    weights = taps(radius, width)
    rows = jnp.arange(length + 2 * radius)[:, None]
    cols = jnp.arange(length)[None, :]
    offset = rows - cols
    inside = (offset >= 0) & (offset <= 2 * radius)
    picked = weights[jnp.clip(offset, 0, 2 * radius)]
    return jnp.where(inside, picked, jnp.zeros_like(picked))


def filter_x(fields, matrix):
    return jnp.einsum("czpy,pq->czqy", fields, matrix, precision=lax.Precision.HIGHEST)


def filter_y(fields, matrix):
    return jnp.einsum("czxp,pq->czxq", fields, matrix, precision=lax.Precision.HIGHEST)


def interpolate(flat_stress, index, weight, size_x, size_y):
    shape = index.shape[1:]
    base = index[0].reshape(-1)
    offsets = weight.reshape(3, -1)
    wx = offsets[0]
    wy = offsets[1]
    wz = offsets[2]
    total = jnp.zeros((6, base.shape[0]), jnp.float32)
    for dz in (0, 1):
        for dx in (0, 1):
            for dy in (0, 1):
                corner = base + dz * size_x * size_y + dx * size_y + dy
                values = jnp.take(flat_stress, corner, axis=1)
                term = (
                    (wz if dz else 1.0 - wz) * (wx if dx else 1.0 - wx) * (wy if dy else 1.0 - wy)
                )
                total = total + term[None, :] * values
    return total.reshape((6,) + shape)


def on_device(velocity, owner, cell_x, cell_y, cell_z, query_weights):
    radius = FW // 2
    size_z = velocity.shape[1]
    size_x = velocity.shape[2]
    size_y = velocity.shape[3]
    layered = padded(velocity, (("gz", 1),), radius)
    band_z = band(size_z, radius, FW)
    band_x = band(size_x, radius, FW)
    band_y = band(size_y, radius, FW)
    fields = []
    for comp in range(3):
        fields.append(
            jnp.einsum("pxy,pz->zxy", layered[comp], band_z, precision=lax.Precision.HIGHEST)
        )
    for first, second in PAIRS:
        product = layered[first] * layered[second]
        fields.append(jnp.einsum("pxy,pz->zxy", product, band_z, precision=lax.Precision.HIGHEST))
    stacked = jnp.stack(fields)
    margined = padded(stacked, (("gx", 2), ("gy", 3)), radius)
    filtered = filter_y(filter_x(margined, band_x), band_y)
    stress = jnp.stack(
        [
            filtered[3 + k] - filtered[first] * filtered[second]
            for k, (first, second) in enumerate(PAIRS)
        ]
    )
    flat_stress = stress.reshape(6, -1)
    bricks_x = lax.axis_size("gx")
    bricks_y = lax.axis_size("gy")
    owners = bricks_x * bricks_y
    count = owner.shape[0]
    capacity = 4 * count // owners
    target = owner[:, 0]
    order = jnp.argsort(target, stable=True)
    sorted_target = target[order]
    tally = jnp.sum(
        (target[:, None] == jnp.arange(owners, dtype=jnp.int32)[None, :]).astype(jnp.int32), axis=0
    )
    starts = jnp.cumsum(tally) - tally
    sorted_rank = jnp.arange(count, dtype=jnp.int32) - starts[sorted_target]
    rank = jnp.zeros((count,), jnp.int32).at[order].set(sorted_rank)
    slot = target * capacity + rank
    local_cell = (cell_z * size_x + cell_x) * size_y + cell_y
    send_index = jnp.zeros((owners * capacity,), jnp.int32).at[slot].set(local_cell)
    send_weight = jnp.zeros((3, owners * capacity), jnp.float32).at[:, slot].set(query_weights)
    values = interpolate(
        flat_stress,
        lax.all_to_all(
            send_index.reshape(1, owners, capacity),
            ("gx", "gy"),
            split_axis=1,
            concat_axis=1,
            tiled=True,
        ),
        lax.all_to_all(
            send_weight.reshape(3, owners, capacity),
            ("gx", "gy"),
            split_axis=1,
            concat_axis=1,
            tiled=True,
        ),
        size_x,
        size_y,
    )
    returned = lax.all_to_all(values, ("gx", "gy"), split_axis=1, concat_axis=1, tiled=True)
    flat_back = returned.reshape(6, owners * capacity)
    return jnp.take(flat_back, slot, axis=1)


def solution(mesh):
    placed = (
        P(None, "gz", "gx", "gy"),
        P(("gx", "gy", "gz"), None),
        P(("gx", "gy", "gz")),
        P(("gx", "gy", "gz")),
        P(("gx", "gy", "gz")),
        P(None, ("gx", "gy", "gz")),
    )
    return jax.shard_map(
        on_device,
        mesh=mesh,
        in_specs=placed,
        out_specs=P(None, ("gx", "gy", "gz")),
        check_vma=False,
    )
```

profile of v0, /device:TPU:1, one launch (start us, length us, event | category | flops | bytes accessed | tf_op | source)
XLA Modules:
  0.0 546.4 jit_solution(7970189455837514659)
XLA Ops:
  7.4 5.1 sort.17
  12.6 4.5 gather_fusion
  17.1 4.3 compare_select_fusion.11
  24.9 4.8 gather_fusion.1
  33.3 5.7 %collective-permute-start.3 = (f32[9,16,16,128]{3,1,2,0:T(8,128)S(1)}, f32[9,16,16,128]{3,1,2,0:T(8,128)}, u32[]{:S(2)}, u32[]{:S(2)}) collective-permute-start(f32[9,16,16,128]{3,1,2,0:T(8,128)S(1)} %fusion.4), channel_id=1, source_target_pairs={{32,0},{64,32},{96,64},{128,96},{160,128},{192,160},{224,192},{0,2... | collective-permute-start | bytes 3538952 | tf_op jit(solution)/shard_map/ppermute | solution.py:20
  38.9 35.9 %select_subtract_fusion = s32[1024]{0:T(1024)S(1)} fusion(pred[1024]{0:T(1024)(128)(4,1)S(1)} %get-tuple-element.67, pred[1024]{0:T(1024)(128)(4,1)S(1)} %get-tuple-element.66, pred[1024]{0:T(1024)(128)(4,1)S(1)} %get-tuple-element.65, pred[1024]{0:T(1024)(128)(4,1)S(1)} %get-tuple-element.64, pred[1024]{0:T(1024)(128)(4,1)S(1)} %get-tuple-element.63, ...), kind=kLoop, calls=%fused_computation.212 | loop fusion | flops 59392 | bytes 66788 | tf_op jit(solution)/shard_map/sub | solution.py:108
  79.8 4.3 scatter_custom_fusion.2
  84.8 9.3 %all-to-all-start.1 = ((s32[1,64,64]{2,0,1:T(1,128)}), s32[1,64,64]{2,0,1:T(1,128)S(1)}, u32[]{:S(2)}, u32[]{:S(2)}) async-start(s32[1,64,64]{2,0,1:T(1,128)} %reshape.232), calls=%async_computation.1 | async-start | bytes 65536 | tf_op jit(solution)/shard_map/all_to_all | solution.py:116
  94.2 209.5 %gather_fusion.2 = f32[20480]{0:T(1024)} fusion(f32[33]{0:T(128)S(1)} %broadcast_divide_fusion, s32[20480]{0:T(1024)S(1)} %fusion.29), kind=kCustom, calls=%fused_computation.10 | custom fusion | bytes 245760 | tf_op jit(solution)/shard_map/gather | solution.py:37
  310.2 10.5 %all-to-all-start = ((f32[64,1,192]{2,1,0:T(1,128)}), f32[64,1,192]{2,1,0:T(1,128)}, u32[]{:S(2)}, u32[]{:S(2)}) async-start(f32[64,1,192]{2,1,0:T(1,128)} %reshape.699), calls=%async_computation | async-start | bytes 131072 | tf_op jit(solution)/shard_map/all_to_all | solution.py:123
  339.6 7.4 %collective-permute-done.5 = f32[9,16,48,16]{2,3,1,0:T(8,128)} collective-permute-done((f32[9,16,48,16]{2,3,1,0:T(8,128)}, f32[9,16,48,16]{2,3,1,0:T(8,128)}, u32[]{:S(2)}, u32[]{:S(2)}) %collective-permute-start.5) | collective-permute-done | bytes 442400 | tf_op jit(solution)/shard_map/ppermute | solution.py:20
  352.8 6.6 %pad_maximum_fusion = f32[9,16,48,160]{3,1,2,0:T(8,128)S(1)} fusion(f32[9,16,48,16]{3,1,2,0:T(8,128)S(1)} %copy.123, f32[9,16,16,128]{3,1,2,0:T(8,128)} %collective-permute-done.3, f32[9,16,16,128]{3,1,2,0:T(8,128)} %copy-done.1, f32[9,16,16,128]{3,1,2,0:T(8,128)} %collective-permute-done.2, f32[9,16,48,16]{3,1,2,0:T(8,128)} %copy.122), kind=kLoop, calls=%fused_computation.15 | loop fusion | flops 4423680 | bytes 8847360 | tf_op jit(solution)/shard_map/concatenate | solution.py:21
  359.4 7.4 %fusion = f32[16,9,16,160]{3,0,2,1:T(8,128)S(1)} fusion(f32[9,16,48,160]{3,1,2,0:T(8,128)S(1)} %pad_maximum_fusion, f32[48,16]{1,0:T(8,128)S(1)} %copy-done.3), kind=kOutput, calls=%fused_computation.16 | convolution fusion | flops 212340480 | bytes 5901312 | tf_op jit(solution)/shard_map/czpy,pq->czqy/dot_general | solution.py:42
  370.3 9.0 %copy.126 = f32[6,32768]{0,1:T(8,128)} copy(f32[6,32768]{1,0:T(8,128)S(1)} %stack.67) | data formatting | bytes 1572864 | tf_op jit(solution)/shard_map/stack | solution.py:89
  379.3 16.6 %gather_fusion.11 = f32[4096,6]{1,0:T(8,128)S(1)} fusion(f32[6,32768]{0,1:T(8,128)} %copy.126, s32[4096]{0:T(1024)S(1)} %copy-done.14), kind=kCustom, calls=%fused_computation.7.clone | custom fusion | bytes 212992 | tf_op jit(solution)/shard_map/jit(_take)/gather | solution.py:61
  396.5 16.6 %gather_fusion.10 = f32[4096,6]{1,0:T(8,128)S(1)} fusion(f32[6,32768]{0,1:T(8,128)} %copy.126, s32[4096]{0:T(1024)S(1)} %copy-done.13), kind=kCustom, calls=%fused_computation.6.clone | custom fusion | bytes 212992 | tf_op jit(solution)/shard_map/jit(_take)/gather | solution.py:61
  413.7 16.8 %gather_fusion.9 = f32[4096,6]{1,0:T(8,128)S(1)} fusion(f32[6,32768]{0,1:T(8,128)} %copy.126, s32[4096]{0:T(1024)S(1)} %copy-done.12), kind=kCustom, calls=%fused_computation.5.clone | custom fusion | bytes 212992 | tf_op jit(solution)/shard_map/jit(_take)/gather | solution.py:61
  431.2 16.6 %gather_fusion.8 = f32[4096,6]{1,0:T(8,128)S(1)} fusion(f32[6,32768]{0,1:T(8,128)} %copy.126, s32[4096]{0:T(1024)S(1)} %copy-done.11), kind=kCustom, calls=%fused_computation.4.clone | custom fusion | bytes 212992 | tf_op jit(solution)/shard_map/jit(_take)/gather | solution.py:61
  448.4 16.6 %gather_fusion.7 = f32[4096,6]{1,0:T(8,128)S(1)} fusion(f32[6,32768]{0,1:T(8,128)} %copy.126, s32[4096]{0:T(1024)S(1)} %copy-done.10), kind=kCustom, calls=%fused_computation.3.clone | custom fusion | bytes 212992 | tf_op jit(solution)/shard_map/jit(_take)/gather | solution.py:61
  465.6 16.6 %gather_fusion.6 = f32[4096,6]{1,0:T(8,128)S(1)} fusion(f32[6,32768]{0,1:T(8,128)} %copy.126, s32[4096]{0:T(1024)S(1)} %copy-done.9), kind=kCustom, calls=%fused_computation.2.clone | custom fusion | bytes 212992 | tf_op jit(solution)/shard_map/jit(_take)/gather | solution.py:61
  482.8 16.6 %gather_fusion.5 = f32[4096,6]{1,0:T(8,128)S(1)} fusion(f32[6,32768]{0,1:T(8,128)} %copy.126, s32[4096]{0:T(1024)S(1)} %copy-done.8), kind=kCustom, calls=%fused_computation.1.clone | custom fusion | bytes 212992 | tf_op jit(solution)/shard_map/jit(_take)/gather | solution.py:61
  500.2 16.6 %gather_fusion.4 = f32[4096,6]{1,0:T(8,128)S(1)} fusion(f32[6,32768]{0,1:T(8,128)} %copy.126, s32[4096]{0:T(1024)S(1)} %copy-done.7), kind=kCustom, calls=%fused_computation.clone | custom fusion | bytes 212992 | tf_op jit(solution)/shard_map/jit(_take)/gather | solution.py:61
  518.7 11.0 %all-to-all-start.2 = ((f32[64,1,384]{2,1,0:T(1,128)}), f32[64,1,384]{2,1,0:T(1,128)S(1)}, u32[]{:S(2)}, u32[]{:S(2)}) async-start(f32[64,1,384]{2,1,0:T(1,128)} %reshape.701), calls=%async_computation.2 | async-start | bytes 196608 | tf_op jit(solution)/shard_map/all_to_all | solution.py:133
  529.8 10.6 %all-to-all-done.2 = f32[64,1,384]{2,1,0:T(1,128)S(1)} async-done(((f32[64,1,384]{2,1,0:T(1,128)}), f32[64,1,384]{2,1,0:T(1,128)S(1)}, u32[]{:S(2)}, u32[]{:S(2)}) %all-to-all-start.2) | async-done | bytes 98336 | tf_op jit(solution)/shard_map/all_to_all | solution.py:133
  (160 shorter events, 66.4 us)
Async XLA Ops:
  1.1 28.6 %collective-permute-start = (f32[3,16,16,128]{3,1,2,0:T(8,128)S(1)}, f32[3,16,16,128]{3,1,2,0:T(8,128)S(1)}, u32[]{:S(2)}, u32[]{:S(2)}) collective-permute-start(f32[3,16,16,128]{3,1,2,0:T(8,128)S(1)} %copy.108), channel_id=1, source_target_pairs={{0,1},{1,2},{2,3},{3,0},{4,5},{5,6},{6,7},{7,4},{8,9},{9,10},{10,1... | collective-permute-start | bytes 1179656 | tf_op jit(solution)/shard_map/ppermute | solution.py:19
  3.3 26.6 %collective-permute-start.1 = (f32[3,16,16,128]{3,1,2,0:T(8,128)S(1)}, f32[3,16,16,128]{3,1,2,0:T(8,128)S(1)}, u32[]{:S(2)}, u32[]{:S(2)}) collective-permute-start(f32[3,16,16,128]{3,1,2,0:T(8,128)S(1)} %copy.108), channel_id=1, source_target_pairs={{1,0},{2,1},{3,2},{0,3},{5,4},{6,5},{7,6},{4,7},{9,8},{10,9},{11,1... | collective-permute-start | bytes 1179656 | tf_op jit(solution)/shard_map/ppermute | solution.py:20
  30.7 49.1 %copy-start.31 = (s32[1024]{0:T(1024)S(1)}, s32[1024]{0:T(1024)}, u32[]{:S(2)}) copy-start(s32[1024]{0:T(1024)} %param.11) | copy-start | bytes 12292
  30.7 49.1 %copy-start.32 = (s32[1024]{0:T(1024)S(1)}, s32[1024]{0:T(1024)}, u32[]{:S(2)}) copy-start(s32[1024]{0:T(1024)} %param.10) | copy-start | bytes 12292
  30.7 49.1 %copy-start.33 = (s32[1024]{0:T(1024)S(1)}, s32[1024]{0:T(1024)}, u32[]{:S(2)}) copy-start(s32[1024]{0:T(1024)} %param.12) | copy-start | bytes 12292
  33.3 289.4 %copy-start.1 = (f32[9,16,16,128]{3,1,2,0:T(8,128)}, f32[9,16,16,128]{3,1,2,0:T(8,128)S(1)}, u32[]{:S(2)}) copy-start(f32[9,16,16,128]{3,1,2,0:T(8,128)S(1)} %fusion.4) | copy-start | bytes 3538948
  33.3 289.4 %collective-permute-start.3 = (f32[9,16,16,128]{3,1,2,0:T(8,128)S(1)}, f32[9,16,16,128]{3,1,2,0:T(8,128)}, u32[]{:S(2)}, u32[]{:S(2)}) collective-permute-start(f32[9,16,16,128]{3,1,2,0:T(8,128)S(1)} %fusion.4), channel_id=1, source_target_pairs={{32,0},{64,32},{96,64},{128,96},{160,128},{192,160},{224,192},{0,2... | collective-permute-start | bytes 3538952 | tf_op jit(solution)/shard_map/ppermute | solution.py:20
  38.9 283.7 %collective-permute-start.2 = (f32[9,16,16,128]{3,1,2,0:T(8,128)S(1)}, f32[9,16,16,128]{3,1,2,0:T(8,128)}, u32[]{:S(2)}, u32[]{:S(2)}) collective-permute-start(f32[9,16,16,128]{3,1,2,0:T(8,128)S(1)} %fusion.4), channel_id=1, source_target_pairs={{0,32},{32,64},{64,96},{96,128},{128,160},{160,192},{192,224},{224... | collective-permute-start | bytes 3538952 | tf_op jit(solution)/shard_map/ppermute | solution.py:19
  79.8 224.9 %copy-start.28 = (s32[1024]{0:T(1024)}, s32[1024]{0:T(1024)S(1)}, u32[]{:S(2)}) copy-start(s32[1024]{0:T(1024)S(1)} %get-tuple-element.69) | copy-start | bytes 12292
  84.8 225.3 %all-to-all-start.1 = ((s32[1,64,64]{2,0,1:T(1,128)}), s32[1,64,64]{2,0,1:T(1,128)S(1)}, u32[]{:S(2)}, u32[]{:S(2)}) async-start(s32[1,64,64]{2,0,1:T(1,128)} %reshape.232), calls=%async_computation.1 | async-start | bytes 65536 | tf_op jit(solution)/shard_map/all_to_all | solution.py:116
  94.2 209.5 %copy-start.27 = (f32[3,1024]{1,0:T(4,128)S(1)}, f32[3,1024]{1,0:T(4,128)}, u32[]{:S(2)}) copy-start(f32[3,1024]{1,0:T(4,128)} %param.13) | copy-start | bytes 36868
  310.2 25.9 %all-to-all-start = ((f32[64,1,192]{2,1,0:T(1,128)}), f32[64,1,192]{2,1,0:T(1,128)}, u32[]{:S(2)}, u32[]{:S(2)}) async-start(f32[64,1,192]{2,1,0:T(1,128)} %reshape.699), calls=%async_computation | async-start | bytes 131072 | tf_op jit(solution)/shard_map/all_to_all | solution.py:123
  330.8 16.2 %collective-permute-start.5 = (f32[9,16,48,16]{2,3,1,0:T(8,128)}, f32[9,16,48,16]{2,3,1,0:T(8,128)}, u32[]{:S(2)}, u32[]{:S(2)}) collective-permute-start(f32[9,16,48,16]{2,3,1,0:T(8,128)} %copy.121), channel_id=1, source_target_pairs={{4,0},{8,4},{12,8},{16,12},{20,16},{24,20},{28,24},{0,28},{5,1},{9... | collective-permute-start | bytes 1327112 | tf_op jit(solution)/shard_map/ppermute | solution.py:20
  333.5 15.9 %collective-permute-start.4 = (f32[9,16,48,16]{2,3,1,0:T(8,128)}, f32[9,16,48,16]{2,3,1,0:T(8,128)}, u32[]{:S(2)}, u32[]{:S(2)}) collective-permute-start(f32[9,16,48,16]{2,3,1,0:T(8,128)} %copy.120), channel_id=1, source_target_pairs={{0,4},{4,8},{8,12},{12,16},{16,20},{20,24},{24,28},{28,0},{1,5},{5... | collective-permute-start | bytes 1327112 | tf_op jit(solution)/shard_map/ppermute | solution.py:19
  413.7 17.5 %copy-start.11 = (s32[4096]{0:T(1024)S(1)}, s32[4096]{0:T(1024)}, u32[]{:S(2)}) copy-start(s32[4096]{0:T(1024)} %get-tuple-element.98) | copy-start | bytes 49156
  500.1 17.4 %copy-start.18 = (f32[4096]{0:T(1024)S(1)}, f32[4096]{0:T(1024)}, u32[]{:S(2)}) copy-start(f32[4096]{0:T(1024)} %get-tuple-element.83) | copy-start | bytes 49156
  500.1 17.4 %copy-start.19 = (f32[4096]{0:T(1024)S(1)}, f32[4096]{0:T(1024)}, u32[]{:S(2)}) copy-start(f32[4096]{0:T(1024)} %get-tuple-element.84) | copy-start | bytes 49156
  500.1 17.4 %copy-start.20 = (f32[4096]{0:T(1024)S(1)}, f32[4096]{0:T(1024)}, u32[]{:S(2)}) copy-start(f32[4096]{0:T(1024)} %get-tuple-element.85) | copy-start | bytes 49156
  500.1 17.4 %copy-start.21 = (f32[4096]{0:T(1024)S(1)}, f32[4096]{0:T(1024)}, u32[]{:S(2)}) copy-start(f32[4096]{0:T(1024)} %get-tuple-element.86) | copy-start | bytes 49156
  500.1 17.4 %copy-start.22 = (f32[4096]{0:T(1024)S(1)}, f32[4096]{0:T(1024)}, u32[]{:S(2)}) copy-start(f32[4096]{0:T(1024)} %get-tuple-element.87) | copy-start | bytes 49156
  500.1 17.4 %copy-start.23 = (pred[4096]{0:T(1024)(128)(4,1)S(1)}, pred[4096]{0:T(1024)(128)(4,1)}, u32[]{:S(2)}) copy-start(pred[4096]{0:T(1024)(128)(4,1)} %get-tuple-element.92) | copy-start | bytes 12292
  500.1 17.4 %copy-start.24 = (pred[4096]{0:T(1024)(128)(4,1)S(1)}, pred[4096]{0:T(1024)(128)(4,1)}, u32[]{:S(2)}) copy-start(pred[4096]{0:T(1024)(128)(4,1)} %get-tuple-element.93) | copy-start | bytes 12292
  517.8 27.1 %copy-start.30 = (pred[1024]{0:T(1024)(128)(4,1)S(1)}, pred[1024]{0:T(1024)(128)(4,1)}, u32[]{:S(2)}) copy-start(pred[1024]{0:T(1024)(128)(4,1)} %get-tuple-element.68) | copy-start | bytes 3076
  518.7 21.6 %all-to-all-start.2 = ((f32[64,1,384]{2,1,0:T(1,128)}), f32[64,1,384]{2,1,0:T(1,128)S(1)}, u32[]{:S(2)}, u32[]{:S(2)}) async-start(f32[64,1,384]{2,1,0:T(1,128)} %reshape.701), calls=%async_computation.2 | async-start | bytes 196608 | tf_op jit(solution)/shard_map/all_to_all | solution.py:133
  (19 other events, 247.5 us)
where the time goes:
time: 556 us; the launch traced here: 546 us
  local copies, waits for them, and re-layouts  409 us (74%)
  other arithmetic  63.9 us (11%)
  starting transfers between devices  41.9 us (8%)
  waiting for transfers between devices  18 us (3%)
  matrix products  12.6 us (2%)
    gather x3, local copies, waits for them, and re-layouts, band(): picked = weights[jnp.clip(offset, 0, 2 * radius)]  214 us
    gather x16, local copies, waits for them, and re-layouts, interpolate(): values = jnp.take(flat_stress, corner, axis=1)  138 us
    sub x1, other arithmetic, on_device(): sorted_rank = jnp.arange(count, dtype=jnp.int32) - starts[sorted_target]  35.9 us
  transfers between devices with their start and end apart: 9, of which 2 were waited for; matrix products, arithmetic and copies ran while one was open for 56% of the time, Pallas kernels for 0%

commit v1 on v0

v1 whole, which is shorter than its diff:
```python
import functools

import jax
import jax.numpy as jnp
import numpy as np
from jax import lax
from jax.experimental import pallas as pl
from jax.experimental.pallas import tpu as pltpu
from jax.sharding import PartitionSpec as P

MESH = pl.DeviceIdType.MESH
F32 = jnp.float32
BF16 = jnp.bfloat16
FW = 32
R = FW // 2
CAP = 64
FIELDS = ((0, None), (0, 0), (1, None), (0, 1), (1, 1), (2, None), (0, 2), (1, 2), (2, 2))
PAIRS = ((0, 0), (0, 1), (0, 2), (1, 1), (1, 2), (2, 2))


def taps():
    offsets = np.arange(2 * R + 1).astype(np.float32) - np.float32(R)
    values = np.exp(np.float32(-6.0) * offsets * offsets / np.float32(FW * FW))
    return (values / values.sum(dtype=np.float32)).astype(np.float32)


def split(x):
    hi = x.astype(BF16)
    lo = (x - hi.astype(F32)).astype(BF16)
    return hi, lo


def np_split(x):
    hi = jnp.asarray(x, F32).astype(BF16)
    lo = (jnp.asarray(x, F32) - hi.astype(F32)).astype(BF16)
    return hi, lo


def tables(by):
    g = taps()

    def band(rows, cols, shift):
        m = np.arange(rows)[:, None] - np.arange(cols)[None, :] + shift
        return np.where((m >= 0) & (m <= 2 * R), g[np.clip(m, 0, 2 * R)], np.float32(0))

    sub = band(3 * R, R, 0).T
    mid = band(by, by, R)
    left = band(R, by, 0)
    right = band(R, by, by + R)
    groups = R // 2
    edge = np.zeros((groups // 2, 2 * 128, 2 * by), np.float32)
    for k in range(groups):
        part = edge[k // 2, :, (k % 2) * by : (k % 2 + 1) * by]
        part[R * k : R * k + R] = left
        part[128 + R * k : 128 + R * k + R] = right
    sh, sl = np_split(sub)
    mh, ml = np_split(mid)
    eh, el = np_split(edge)
    return (
        jnp.concatenate([sh, sl, sh], axis=1),
        jnp.concatenate([mh, mh], axis=0),
        ml,
        eh,
        el,
    )


def dot(a, b):
    return jnp.dot(a, b, preferred_element_type=F32)


def kernel(
    sizes,
    v_ref, own_ref, cx_ref, cy_ref, cz_ref, qw_ref, sub_ref, mid_ref, midl_ref, eh_hbm, el_hbm,
    out_ref,
    u, xb, yb, zf, pack, halo, eh, el,
    sendq, gotq, passq, haveq, rows, w1h, w1l, wyb,
    sth, stl, vals, sendr, gotr, passr, haver, onehot, rankhot,
    s1, r1, s2, r2, s3, r3, sa, ra, sb, rb, sc, rc, sd, rd, lsem,
):
    nx, ny, nz = sizes
    g = [float(t) for t in taps()]
    mx, my, mz = lax.axis_index("gx"), lax.axis_index("gy"), lax.axis_index("gz")
    par = lax.rem(my, 2)
    owners = nx * ny
    count = own_ref.shape[1]

    def shifted(first, step):
        on_x = par if first else 1 - par
        on_z = 1 - on_x
        return (
            lax.rem(mx + on_x * (step % nx), nx),
            my,
            lax.rem(mz + on_z * (step % nz), nz),
        )

    def y_peer(step):
        return (mx, lax.rem(my + step % ny, ny), mz)

    def x_peer(step):
        return (lax.rem(mx + step % nx, nx), my, mz)

    def remote(src, dst, ssem, rsem, dev):
        return pltpu.make_async_remote_copy(
            src_ref=src, dst_ref=dst, send_sem=ssem, recv_sem=rsem, device_id=dev, device_id_type=MESH
        )

    load_eh = pltpu.make_async_copy(eh_hbm, eh, lsem.at[0])
    load_el = pltpu.make_async_copy(el_hbm, el, lsem.at[1])
    load_eh.start()
    load_el.start()

    @pl.when(par == 0)
    def _():
        for c in range(3):
            u[c, R : 2 * R] = v_ref[c].reshape(R, R, 128)

    @pl.when(par == 1)
    def _():
        for c in range(3):
            for b in range(R):
                u[c, R + b] = v_ref[c, pl.ds(b, R, stride=R), :]

    barrier = pltpu.get_barrier_semaphore()
    for step in range(1, nx):
        pl.semaphore_signal(barrier, inc=1, device_id=x_peer(step), device_id_type=MESH)
    for step in range(1, ny):
        pl.semaphore_signal(barrier, inc=1, device_id=y_peer(step), device_id_type=MESH)
    for step in (1, nz - 1):
        pl.semaphore_signal(
            barrier, inc=1, device_id=(mx, my, lax.rem(mz + step, nz)), device_id_type=MESH
        )
    pl.semaphore_wait(barrier, nx - 1 + ny - 1 + 2)

    def first_copies(c):
        src = u.at[c, pl.ds(R, R)]
        return (
            remote(src, u.at[c, pl.ds(0, R)], s1.at[c, 0], r1.at[c, 0], shifted(True, 1)),
            remote(src, u.at[c, pl.ds(2 * R, R)], s1.at[c, 1], r1.at[c, 1], shifted(True, -1)),
        )

    def second_copies(f):
        src = xb.at[f, :, pl.ds(R, R)]
        return (
            remote(src, xb.at[f, :, pl.ds(0, R)], s2.at[f, 0], r2.at[f, 0], shifted(False, 1)),
            remote(src, xb.at[f, :, pl.ds(2 * R, R)], s2.at[f, 1], r2.at[f, 1], shifted(False, -1)),
        )

    def y_copies(f):
        return (
            remote(pack.at[0, f], halo.at[1, f], s3.at[f, 0], r3.at[f, 0], y_peer(-1)),
            remote(pack.at[1, f], halo.at[0, f], s3.at[f, 1], r3.at[f, 1], y_peer(1)),
        )

    def exchange(n, peer_of, me, src, dst, ssem, rsem):
        copies = []
        for step in range(1, n):
            copies.append(
                remote(
                    src.at[lax.rem(me + step, n)], dst.at[me], ssem.at[step], rsem.at[step], peer_of(step)
                )
            )
        return copies

    for c in range(3):
        for copy in first_copies(c):
            copy.start()

    bits_y = ny.bit_length() - 1
    own = own_ref[...]
    target = (own & (ny - 1)) * nx + (own >> bits_y)
    hot = (lax.broadcasted_iota(jnp.int32, (owners, count), 0) == target).astype(F32)
    onehot[...] = hot.astype(BF16)
    earlier = (
        lax.broadcasted_iota(jnp.int32, (128, 128), 0) < lax.broadcasted_iota(jnp.int32, (128, 128), 1)
    ).astype(BF16)
    carry = jnp.zeros((owners, 1), F32)
    ranks = []
    for block in range(count // 128):
        part = hot[:, block * 128 : block * 128 + 128]
        before = dot(part.astype(BF16), earlier) + carry
        ranks.append(jnp.sum(part * before, axis=0, keepdims=True))
        carry = carry + jnp.sum(part, axis=1, keepdims=True)
    rank = jnp.concatenate(ranks, axis=1)
    slot = lax.broadcasted_iota(jnp.int32, (CAP, count), 0).astype(F32) == rank
    rankhot[...] = slot.astype(F32)
    cell = (cz_ref[...] * R + cx_ref[...]) * 128 + cy_ref[...]

    def pieces(w):
        p0 = w.astype(BF16).astype(F32)
        p1 = (w - p0).astype(BF16).astype(F32)
        p2 = w - p0 - p1
        return p0, p1, p2

    wx = pieces(qw_ref[0:1, :])
    wy = pieces(qw_ref[1:2, :])
    wz = pieces(qw_ref[2:3, :])
    cell_hi = (cell >> 8).astype(F32)
    cell_lo = (cell & 255).astype(F32)
    zero = jnp.zeros_like(cell_lo)
    order = [
        cell_hi, wx[0], cell_lo, wx[1], zero, wx[2],
        wy[0], wz[0], wy[1], wz[1], wy[2], wz[2],
    ]
    placed = jnp.concatenate(
        [jnp.where(slot, p, jnp.zeros_like(p)).astype(BF16) for p in order], axis=0
    )
    spread = lax.dot_general(
        onehot[...], placed, (((1,), (1,)), ((), ())), preferred_element_type=F32
    )
    lane = lax.broadcasted_iota(jnp.int32, (1, 128), 1)
    scale = jnp.where(lane < CAP, 256.0, 1.0)
    head = spread[:, 0:128] * scale + spread[:, 128:256] + spread[:, 256:384]
    tail = spread[:, 384:512] + spread[:, 512:640] + spread[:, 640:768]
    for j in range(ny):
        sendq[j, 0] = head[j * nx : (j + 1) * nx]
        sendq[j, 1] = tail[j * nx : (j + 1) * nx]
    out_y = exchange(ny, y_peer, my, sendq, gotq, sa, ra)
    for copy in out_y:
        copy.start()
    gotq[my] = sendq[my]

    def first_filter(f):
        i, j = FIELDS[f]

        def chunk(n, _):
            bs = pl.multiple_of((n // 2) * 8, 8)
            h = (n % 2) * 8
            x = u[i, pl.ds(h, 40), pl.ds(bs, 8), :]
            if j is not None:
                x = x * u[j, pl.ds(h, 40), pl.ds(bs, 8), :]
            acc = x[R : R + 8] * g[R]
            for d in range(1, R + 1):
                acc = acc + (x[R - d : R + 8 - d] + x[R + d : R + 8 + d]) * g[R + d]
            xb[f, pl.ds(h, 8), pl.ds(R + bs, 8), :] = acc
            return 0

        lax.fori_loop(0, 4, chunk, 0)
        for copy in second_copies(f):
            copy.start()

    def pass_on():
        for copy in out_y:
            copy.wait_recv()
        for i in range(nx):
            for k in range(2):
                passq[i, k] = gotq[:, k, i, :]
        out_x = exchange(nx, x_peer, mx, passq, haveq, sb, rb)
        for copy in out_x:
            copy.start()
        haveq[mx] = passq[mx]
        return out_x

    field = 0
    for c in range(3):
        for copy in first_copies(c):
            copy.wait_recv()
        for _ in range(c + 2):
            first_filter(field)
            field += 1
        if c == 0:
            out_x = pass_on()

    for copy in out_x:
        copy.wait_recv()
    half = owners // 2
    table = [
        jnp.concatenate([haveq[i, k] for i in range(nx)], axis=0) for k in range(2)
    ]
    low = lane < CAP

    def paired(x, second):
        top, bottom = x[:half], x[half:]
        if second:
            return jnp.where(low, pltpu.roll(top, CAP, 1), bottom)
        return jnp.where(low, top, pltpu.roll(bottom, CAP, 1))

    q_cell = paired(table[0], False).astype(jnp.int32)
    q_wx = paired(table[0], True)
    q_wy = paired(table[1], False)
    q_wz = paired(table[1], True)
    q_cz = (q_cell >> 11).astype(F32)
    q_cx = ((q_cell >> 7) & (R - 1)).astype(F32)
    z_first = par == 0
    rows[0] = jnp.where(z_first, q_cz, q_cx)
    rows[1] = jnp.where(z_first, q_cx, q_cz)
    rows[2] = (q_cell & 127).astype(F32)
    rows[3] = jnp.where(z_first, q_wz, q_wx)
    rows[4] = jnp.where(z_first, q_wx, q_wz)
    rows[5] = q_wy
    chunks = owners * CAP // 256

    def weights(n, _):
        def row(k):
            return jnp.concatenate([rows[k, pl.ds(2 * n, 1), :], rows[k, pl.ds(2 * n + 1, 1), :]], axis=1)

        def hat(size, at, w):
            index = lax.broadcasted_iota(jnp.int32, (size, 256), 0).astype(F32)
            return jnp.where(index == at, 1.0 - w, jnp.where(index == at + 1.0, w, 0.0))

        wa = hat(R, row(0), row(3))
        wb = hat(R, row(1), row(4))
        for a in range(R):
            hi, lo = split(wa[a : a + 1] * wb)
            w1h[n, R * a : R * a + R, :] = hi
            w1l[n, R * a : R * a + R, :] = lo
        wyb[n] = hat(128, row(2), row(5))
        return 0

    lax.fori_loop(0, chunks, weights, 0)

    group = lax.broadcasted_iota(jnp.int32, (1, 128), 1) // R

    def second_filter(f, _):
        for copy in second_copies(f):
            copy.wait_recv()

        def pair(n, _):
            x = jnp.concatenate([xb[f, 2 * n], xb[f, 2 * n + 1]], axis=1)
            hi, lo = split(x)
            o = dot(sub_ref[...], jnp.concatenate([hi, hi, lo], axis=0))
            yb[f, pl.ds(pl.multiple_of(32 * n, 32), R), :] = o[:, :128]
            yb[f, pl.ds(pl.multiple_of(32 * n, 32) + R, R), :] = o[:, 128:]
            return 0

        lax.fori_loop(0, R // 2, pair, 0)
        for e in range(2):
            first = jnp.zeros((R, 128), F32)
            last = jnp.zeros((R, 128), F32)
            for k in range(R // 2):
                turned = yb[f, pl.ds(2 * k + e, R, stride=R), :]
                first = jnp.where(group == k, pltpu.roll(turned, R * k, 1) if k else turned, first)
                last = jnp.where(group == k, pltpu.roll(turned, (R * k + R) % 128, 1) if k < 7 else turned, last)
            pack[0, f, e] = first
            pack[1, f, e] = last
        for copy in y_copies(f):
            copy.start()
        hi, lo = split(yb[f])
        zf[f] = dot(jnp.concatenate([hi, lo], axis=1), mid_ref[...]) + dot(hi, midl_ref[...])
        return 0

    lax.fori_loop(0, 9, second_filter, 0)

    load_eh.wait()
    load_el.wait()

    def wait_y(f, _):
        for copy in y_copies(f):
            copy.wait_recv()
        return 0

    lax.fori_loop(0, 9, wait_y, 0)
    edges = jnp.concatenate([halo[0].reshape(9 * 32, 128), halo[1].reshape(9 * 32, 128)], axis=1)
    eg_hi, eg_lo = split(edges)
    for kk in range(R // 4):
        part = dot(eg_hi, eh[kk]) + dot(eg_lo, eh[kk]) + dot(eg_hi, el[kk])
        for k in range(2):
            at = 32 * (2 * kk + k)
            zf[:, at : at + 32, :] += part[:, 128 * k : 128 * k + 128].reshape(9, 32, 128)

    for p, (i, j) in enumerate(PAIRS):
        tau = zf[FIELDS.index((i, j))] - zf[FIELDS.index((i, None))] * zf[FIELDS.index((j, None))]
        hi, lo = split(tau.T)
        sth[128 * p : 128 * p + 128] = hi
        stl[128 * p : 128 * p + 128] = lo

    def interpolate(n, _):
        high = w1h[n]
        acc = dot(sth[...], high) + dot(stl[...], high) + dot(sth[...], w1l[n])
        wys = wyb[n]
        for p in range(6):
            v = jnp.sum(acc[128 * p : 128 * p + 128] * wys, axis=0, keepdims=True)
            vals[p, pl.ds(2 * n, 1), :] = v[:, :128]
            vals[p, pl.ds(2 * n + 1, 1), :] = v[:, 128:]
        return 0

    lax.fori_loop(0, chunks, interpolate, 0)

    for k in range(3):
        a, b = vals[2 * k], vals[2 * k + 1]
        top = jnp.where(low, a, pltpu.roll(b, CAP, 1))
        bottom = jnp.where(low, pltpu.roll(a, CAP, 1), b)
        both = jnp.concatenate([top, bottom], axis=0)
        for i in range(nx):
            sendr[i, k] = both[i * ny : (i + 1) * ny]
    back_x = exchange(nx, x_peer, mx, sendr, gotr, sc, rc)
    for copy in back_x:
        copy.start()
    gotr[mx] = sendr[mx]
    for copy in back_x:
        copy.wait_recv()
    for j in range(ny):
        for k in range(3):
            passr[j, k] = gotr[:, k, j, :]
    back_y = exchange(ny, y_peer, my, passr, haver, sd, rd)
    for copy in back_y:
        copy.start()
    haver[my] = passr[my]
    for copy in back_y:
        copy.wait_recv()
    pad = jnp.zeros((128 - owners, 128), F32)
    hot_pad = jnp.concatenate([onehot[...], jnp.zeros((128 - owners, count), BF16)], axis=0)
    hot_two = jnp.concatenate([hot_pad, hot_pad], axis=0)
    at_rank = rankhot[...]
    for k in range(3):
        piece = jnp.concatenate([haver[j, k] for j in range(ny)] + [pad], axis=0)
        hi, lo = split(piece.T)
        picked = dot(jnp.concatenate([hi, lo], axis=1), hot_two)
        for h in range(2):
            out_ref[2 * k + h : 2 * k + h + 1, :] = jnp.sum(
                picked[CAP * h : CAP * h + CAP] * at_rank, axis=0, keepdims=True
            )

    for c in range(3):
        for copy in first_copies(c):
            copy.wait_send()

    def wait_sends(f, _):
        for copy in second_copies(f) + y_copies(f):
            copy.wait_send()
        return 0

    lax.fori_loop(0, 9, wait_sends, 0)
    for copy in out_y + out_x + back_x + back_y:
        copy.wait_send()


def on_device(sizes, velocity, owner, cell_x, cell_y, cell_z, query_weights):
    nx, ny, nz = sizes
    count = owner.shape[0]
    owners = nx * ny
    half = owners // 2
    chunks = owners * CAP // 256
    vmem = pl.BlockSpec(memory_space=pltpu.VMEM)
    hbm = pl.BlockSpec(memory_space=pl.ANY)
    dma = pltpu.SemaphoreType.DMA
    return pl.pallas_call(
        functools.partial(kernel, sizes),
        out_shape=jax.ShapeDtypeStruct((6, count), F32),
        in_specs=[vmem] * 9 + [hbm] * 2,
        out_specs=vmem,
        scratch_shapes=[
            pltpu.VMEM((3, 3 * R, R, 128), F32),
            pltpu.VMEM((9, R, 3 * R, 128), F32),
            pltpu.VMEM((9, R * R, 128), F32),
            pltpu.VMEM((9, R * R, 128), F32),
            pltpu.VMEM((2, 9, 2, R, 128), F32),
            pltpu.VMEM((2, 9, 2, R, 128), F32),
            pltpu.VMEM((4, 256, 256), BF16),
            pltpu.VMEM((4, 256, 256), BF16),
            pltpu.VMEM((ny, 2, nx, 128), F32),
            pltpu.VMEM((ny, 2, nx, 128), F32),
            pltpu.VMEM((nx, 2, ny, 128), F32),
            pltpu.VMEM((nx, 2, ny, 128), F32),
            pltpu.VMEM((6, half, 128), F32),
            pltpu.VMEM((chunks, 256, 256), BF16),
            pltpu.VMEM((chunks, 256, 256), BF16),
            pltpu.VMEM((chunks, 128, 256), F32),
            pltpu.VMEM((768, 256), BF16),
            pltpu.VMEM((768, 256), BF16),
            pltpu.VMEM((6, half, 128), F32),
            pltpu.VMEM((nx, 3, ny, 128), F32),
            pltpu.VMEM((nx, 3, ny, 128), F32),
            pltpu.VMEM((ny, 3, nx, 128), F32),
            pltpu.VMEM((ny, 3, nx, 128), F32),
            pltpu.VMEM((owners, count), BF16),
            pltpu.VMEM((CAP, count), F32),
            dma((3, 2)), dma((3, 2)),
            dma((9, 2)), dma((9, 2)),
            dma((9, 2)), dma((9, 2)),
            dma((ny,)), dma((ny,)),
            dma((nx,)), dma((nx,)),
            dma((nx,)), dma((nx,)),
            dma((ny,)), dma((ny,)),
            dma((2,)),
        ],
        compiler_params=pltpu.CompilerParams(
            collective_id=0, has_side_effects=True, vmem_limit_bytes=48 * 1024 * 1024
        ),
    )(
        velocity.reshape(3, R * R, 128),
        owner.reshape(1, count),
        cell_x.reshape(1, count),
        cell_y.reshape(1, count),
        cell_z.reshape(1, count),
        query_weights,
        *tables(velocity.shape[3]),
    )


def solution(mesh):
    sizes = (mesh.shape["gx"], mesh.shape["gy"], mesh.shape["gz"])
    placed = (
        P(None, "gz", "gx", "gy"),
        P(("gx", "gy", "gz"), None),
        P(("gx", "gy", "gz")),
        P(("gx", "gy", "gz")),
        P(("gx", "gy", "gz")),
        P(None, ("gx", "gy", "gz")),
    )
    return jax.shard_map(
        functools.partial(on_device, sizes),
        mesh=mesh,
        in_specs=placed,
        out_specs=P(None, ("gx", "gy", "gz")),
        check_vma=False,
    )
```

time: 556 us -> 68.9 us (0.12); the launches traced: 546 us -> 68.4 us
  local copies, waits for them, and re-layouts: 409 us -> 9.45 us
  other arithmetic: 63.9 us -> 0 us
  Pallas kernels: 0 us -> 58.9 us
  starting transfers between devices: 41.9 us -> 0 us
  waiting for transfers between devices: 18 us -> 0 us
  matrix products: 12.6 us -> 0 us
    gather x25 -> x0, local copies, waits for them, and re-layouts: 362 us -> none  [the longest x3 214 us: band(): picked = weights[jnp.clip(offset, 0, 2 * radius)]]
    pallas_call x0 -> x1, Pallas kernels: none -> 58.9 us  [on_device(): pl.pallas_call(functools.partial(kernel, sizes), out_shape=jax.ShapeDtype...]
    sub x3 -> x0, other arithmetic: 36 us -> none  [the longest x1 35.9 us: on_device(): sorted_rank = jnp.arange(count, dtype=jnp.int32) - starts[sorted_target]]
    all_to_all x3 -> x0, starting transfers between devices: 30.8 us -> none  [the longest x1 11 us: on_device(): lax.all_to_all(values, ('gx', 'gy'), split_axis=1, concat_axis=1, tiled=T...]
    scatter x3 -> x0, local copies, waits for them, and re-layouts: 12.6 us -> none  [the longest x1 4.33 us: on_device(): jnp.zeros((owners * capacity,), jnp.int32).at[slot].set(local_cell)]
    dot_general x11 -> x0, matrix products: 12.6 us -> none  [the longest x1 7.4 us: filter_x(): jnp.einsum('czpy,pq->czqy', fields, matrix, precision=lax.Precision.HIGHEST)]
    ppermute x6 -> x0, starting transfers between devices: 11.1 us -> none  [the longest x3 7.71 us: padded(): after = lax.ppermute(initial, axis, down)]
    all_to_all x3 -> x0, waiting for transfers between devices: 10.6 us -> none  [the longest x1 10.6 us: on_device(): lax.all_to_all(values, ('gx', 'gy'), split_axis=1, concat_axis=1, tiled=T...]
  transfers between devices with their start and end apart: 9 -> 0, of which waited for: 2 -> 0; matrix products, arithmetic and copies ran while one was open for 56% -> 0% of each run, Pallas kernels for 0% -> 0%
where the time goes in v1:
time: 68.9 us; the launch traced here: 68.4 us
  Pallas kernels  58.9 us (85%)
  local copies, waits for them, and re-layouts  9.45 us (14%)
    pallas_call x1, Pallas kernels, on_device(): pl.pallas_call(functools.partial(kernel, sizes), out_shape=jax.ShapeDtype...  58.9 us
    unnamed x23, local copies, waits for them, and re-layouts  9.45 us

profile of v1, /device:TPU:1, one launch (start us, length us, event | category | flops | bytes accessed | tf_op | source)
XLA Modules:
  0.0 68.4 jit_solution(12622334921555054698)
XLA Ops:
  0.0 0.0 copy-start.6
  0.0 0.7 %copy-done.6 = bf16[16,144]{1,0:T(8,128)(2,1)S(1)} copy-done((bf16[16,144]{1,0:T(8,128)(2,1)S(1)}, bf16[16,144]{1,0:T(8,128)(2,1)}, u32[]{:S(2)}) %copy-start.6) | copy-done | bytes 4632
  0.7 0.0 copy-start
  0.7 1.0 %copy-done = bf16[4,256,256]{2,1,0:T(8,128)(2,1)S(1)} copy-done((bf16[4,256,256]{2,1,0:T(8,128)(2,1)S(1)}, bf16[4,256,256]{2,1,0:T(8,128)(2,1)}, u32[]{:S(2)}) %copy-start) | copy-done | bytes 524312
  1.7 0.0 copy-start.1
  1.7 1.0 %copy-done.1 = bf16[4,256,256]{2,1,0:T(8,128)(2,1)S(1)} copy-done((bf16[4,256,256]{2,1,0:T(8,128)(2,1)S(1)}, bf16[4,256,256]{2,1,0:T(8,128)(2,1)}, u32[]{:S(2)}) %copy-start.1) | copy-done | bytes 524312
  2.8 0.0 copy-start.2
  2.8 1.0 %copy-done.2 = f32[3,16,16,128]{3,2,1,0:T(8,128)S(1)} copy-done((f32[3,16,16,128]{3,2,1,0:T(8,128)S(1)}, f32[3,16,16,128]{3,2,1,0:T(8,128)}, u32[]{:S(2)}) %copy-start.2) | copy-done | bytes 393240
  3.8 0.0 copy-start.3
  3.8 0.8 %copy-done.3 = bf16[256,128]{1,0:T(8,128)(2,1)S(1)} copy-done((bf16[256,128]{1,0:T(8,128)(2,1)S(1)}, bf16[256,128]{1,0:T(8,128)(2,1)}, u32[]{:S(2)}) %copy-start.3) | copy-done | bytes 65560
  4.6 0.0 copy-start.4
  4.6 0.8 %copy-done.4 = bf16[128,128]{1,0:T(8,128)(2,1)S(1)} copy-done((bf16[128,128]{1,0:T(8,128)(2,1)S(1)}, bf16[128,128]{1,0:T(8,128)(2,1)}, u32[]{:S(2)}) %copy-start.4) | copy-done | bytes 32792
  5.4 0.0 copy-start.5
  5.4 0.7 %copy-done.5 = f32[3,1024]{1,0:T(4,128)S(1)} copy-done((f32[3,1024]{1,0:T(4,128)S(1)}, f32[3,1024]{1,0:T(4,128)}, u32[]{:S(2)}) %copy-start.5) | copy-done | bytes 12312
  6.1 0.0 copy-start.7
  6.1 0.7 %copy-done.7 = s32[1024,1]{0,1:T(1,128)S(1)} copy-done((s32[1024,1]{0,1:T(1,128)S(1)}, s32[1024,1]{0,1:T(1,128)}, u32[]{:S(2)}) %copy-start.7) | copy-done | bytes 4120
  6.8 0.0 copy-start.8
  6.8 0.7 %copy-done.8 = s32[1024]{0:T(1024)S(1)} copy-done((s32[1024]{0:T(1024)S(1)}, s32[1024]{0:T(1024)}, u32[]{:S(2)}) %copy-start.8) | copy-done | bytes 4120
  7.5 0.0 copy-start.9
  7.5 0.7 %copy-done.9 = s32[1024]{0:T(1024)S(1)} copy-done((s32[1024]{0:T(1024)S(1)}, s32[1024]{0:T(1024)}, u32[]{:S(2)}) %copy-start.9) | copy-done | bytes 4120
  8.2 0.0 copy-start.10
  8.2 0.7 %copy-done.10 = s32[1024]{0:T(1024)S(1)} copy-done((s32[1024]{0:T(1024)S(1)}, s32[1024]{0:T(1024)}, u32[]{:S(2)}) %copy-start.10) | copy-done | bytes 4120
  8.8 58.9 %shard_map.118 = f32[6,1024]{1,0:T(8,128)S(1)} custom-call(f32[3,256,128]{2,1,0:T(8,128)S(1)} %bitcast.5, s32[1,1024]{1,0:T(1,128)S(1)} %bitcast.6, s32[1,1024]{1,0:T(1,128)S(1)} %bitcast.7, s32[1,1024]{1,0:T(1,128)S(1)} %bitcast.8, s32[1,1024]{1,0:T(1,128)S(1)} %bitcast.9, f32[3,1024]{1,0:T(4,128)S(1)} %copy-done.5, bf16[16,144]{1,0:T(8,128)(2,1)S(1)} %copy-done.6, ...), custom_call_target="tpu_custom_call" | custom-call | tf_op jit(solution)/shard_map/pallas_call | solution.py:437
  67.8 0.6 copy.14
Async XLA Ops:
  0.0 0.7 %copy-start.6 = (bf16[16,144]{1,0:T(8,128)(2,1)S(1)}, bf16[16,144]{1,0:T(8,128)(2,1)}, u32[]{:S(2)}) copy-start(bf16[16,144]{1,0:T(8,128)(2,1)} %constant.13.sub_ref) | copy-start | bytes 13828
  0.7 1.0 %copy-start = (bf16[4,256,256]{2,1,0:T(8,128)(2,1)S(1)}, bf16[4,256,256]{2,1,0:T(8,128)(2,1)}, u32[]{:S(2)}) copy-start(bf16[4,256,256]{2,1,0:T(8,128)(2,1)} %constant.22.el_hbm) | copy-start | bytes 1572868
  1.7 1.0 %copy-start.1 = (bf16[4,256,256]{2,1,0:T(8,128)(2,1)S(1)}, bf16[4,256,256]{2,1,0:T(8,128)(2,1)}, u32[]{:S(2)}) copy-start(bf16[4,256,256]{2,1,0:T(8,128)(2,1)} %constant.19.eh_hbm) | copy-start | bytes 1572868
  2.8 1.0 %copy-start.2 = (f32[3,16,16,128]{3,2,1,0:T(8,128)S(1)}, f32[3,16,16,128]{3,2,1,0:T(8,128)}, u32[]{:S(2)}) copy-start(f32[3,16,16,128]{3,2,1,0:T(8,128)} %param.12) | copy-start | bytes 1179652
  3.8 0.8 %copy-start.3 = (bf16[256,128]{1,0:T(8,128)(2,1)S(1)}, bf16[256,128]{1,0:T(8,128)(2,1)}, u32[]{:S(2)}) copy-start(bf16[256,128]{1,0:T(8,128)(2,1)} %constant.15.mid_ref) | copy-start | bytes 196612
  4.6 0.8 %copy-start.4 = (bf16[128,128]{1,0:T(8,128)(2,1)S(1)}, bf16[128,128]{1,0:T(8,128)(2,1)}, u32[]{:S(2)}) copy-start(bf16[128,128]{1,0:T(8,128)(2,1)} %constant.18.midl_ref) | copy-start | bytes 98308
  5.4 0.7 %copy-start.5 = (f32[3,1024]{1,0:T(4,128)S(1)}, f32[3,1024]{1,0:T(4,128)}, u32[]{:S(2)}) copy-start(f32[3,1024]{1,0:T(4,128)} %qw_ref.1) | copy-start | bytes 36868
  6.1 0.7 %copy-start.7 = (s32[1024,1]{0,1:T(1,128)S(1)}, s32[1024,1]{0,1:T(1,128)}, u32[]{:S(2)}) copy-start(s32[1024,1]{0,1:T(1,128)} %param.13) | copy-start | bytes 12292
  6.8 0.7 %copy-start.8 = (s32[1024]{0:T(1024)S(1)}, s32[1024]{0:T(1024)}, u32[]{:S(2)}) copy-start(s32[1024]{0:T(1024)} %param.14) | copy-start | bytes 12292
  7.5 0.7 %copy-start.9 = (s32[1024]{0:T(1024)S(1)}, s32[1024]{0:T(1024)}, u32[]{:S(2)}) copy-start(s32[1024]{0:T(1024)} %param.15) | copy-start | bytes 12292
  8.2 0.7 %copy-start.10 = (s32[1024]{0:T(1024)S(1)}, s32[1024]{0:T(1024)}, u32[]{:S(2)}) copy-start(s32[1024]{0:T(1024)} %param.16) | copy-start | bytes 12292

commit v2 on v1

--- a/solution.py
+++ b/solution.py
@@ -71,8 +71,9 @@
 
 def kernel(
     sizes,
-    v_ref, own_ref, cx_ref, cy_ref, cz_ref, qw_ref, sub_ref, mid_ref, midl_ref, eh_hbm, el_hbm,
+    v_hbm, own_hbm, cx_hbm, cy_hbm, cz_hbm, qw_hbm, sub_hbm, mid_hbm, midl_hbm, eh_hbm, el_hbm,
     out_ref,
+    v_ref, own_ref, cx_ref, cy_ref, cz_ref, qw_ref, sub_ref, mid_ref, midl_ref,
     u, xb, yb, zf, pack, halo, eh, el,
     sendq, gotq, passq, haveq, rows, w1h, w1l, wyb,
     sth, stl, vals, sendr, gotr, passr, haver, onehot, rankhot,
@@ -105,21 +106,26 @@
             src_ref=src, dst_ref=dst, send_sem=ssem, recv_sem=rsem, device_id=dev, device_id_type=MESH
         )
 
-    load_eh = pltpu.make_async_copy(eh_hbm, eh, lsem.at[0])
-    load_el = pltpu.make_async_copy(el_hbm, el, lsem.at[1])
-    load_eh.start()
-    load_el.start()
-
-    @pl.when(par == 0)
-    def _():
-        for c in range(3):
-            u[c, R : 2 * R] = v_ref[c].reshape(R, R, 128)
-
-    @pl.when(par == 1)
-    def _():
-        for c in range(3):
-            for b in range(R):
-                u[c, R + b] = v_ref[c, pl.ds(b, R, stride=R), :]
+    loads = [
+        pltpu.make_async_copy(src, dst, lsem.at[number])
+        for number, (src, dst) in enumerate(
+            (
+                (v_hbm, v_ref),
+                (own_hbm, own_ref),
+                (cx_hbm, cx_ref),
+                (cy_hbm, cy_ref),
+                (cz_hbm, cz_ref),
+                (qw_hbm, qw_ref),
+                (sub_hbm, sub_ref),
+                (mid_hbm, mid_ref),
+                (midl_hbm, midl_ref),
+                (eh_hbm, eh),
+                (el_hbm, el),
+            )
+        )
+    ]
+    for load in loads:
+        load.start()
 
     barrier = pltpu.get_barrier_semaphore()
     for step in range(1, nx):
@@ -130,6 +136,20 @@
         pl.semaphore_signal(
             barrier, inc=1, device_id=(mx, my, lax.rem(mz + step, nz)), device_id_type=MESH
         )
+
+    loads[0].wait()
+
+    @pl.when(par == 0)
+    def _():
+        for c in range(3):
+            u[c, R : 2 * R] = v_ref[c].reshape(R, R, 128)
+
+    @pl.when(par == 1)
+    def _():
+        for c in range(3):
+            for b in range(R):
+                u[c, R + b] = v_ref[c, pl.ds(b, R, stride=R), :]
+
     pl.semaphore_wait(barrier, nx - 1 + ny - 1 + 2)
 
     def first_copies(c):
@@ -166,6 +186,8 @@
         for copy in first_copies(c):
             copy.start()
 
+    for load in loads[1:6]:
+        load.wait()
     bits_y = ny.bit_length() - 1
     own = own_ref[...]
     target = (own & (ny - 1)) * nx + (own >> bits_y)
@@ -310,6 +332,8 @@
     lax.fori_loop(0, chunks, weights, 0)
 
     group = lax.broadcasted_iota(jnp.int32, (1, 128), 1) // R
+    for load in loads[6:9]:
+        load.wait()
 
     def second_filter(f, _):
         for copy in second_copies(f):
@@ -341,8 +365,8 @@
 
     lax.fori_loop(0, 9, second_filter, 0)
 
-    load_eh.wait()
-    load_el.wait()
+    for load in loads[9:]:
+        load.wait()
 
     def wait_y(f, _):
         for copy in y_copies(f):
@@ -432,14 +456,21 @@
     half = owners // 2
     chunks = owners * CAP // 256
     vmem = pl.BlockSpec(memory_space=pltpu.VMEM)
-    hbm = pl.BlockSpec(memory_space=pl.ANY)
+    hbm = pl.BlockSpec(memory_space=pltpu.HBM)
+    row = pltpu.VMEM((1, count), jnp.int32)
     dma = pltpu.SemaphoreType.DMA
     return pl.pallas_call(
         functools.partial(kernel, sizes),
         out_shape=jax.ShapeDtypeStruct((6, count), F32),
-        in_specs=[vmem] * 9 + [hbm] * 2,
+        in_specs=[hbm] * 11,
         out_specs=vmem,
         scratch_shapes=[
+            pltpu.VMEM((3, R * R, 128), F32),
+            row, row, row, row,
+            pltpu.VMEM((3, count), F32),
+            pltpu.VMEM((R, 9 * R), BF16),
+            pltpu.VMEM((256, 128), BF16),
+            pltpu.VMEM((128, 128), BF16),
             pltpu.VMEM((3, 3 * R, R, 128), F32),
             pltpu.VMEM((9, R, 3 * R, 128), F32),
             pltpu.VMEM((9, R * R, 128), F32),
@@ -472,10 +503,10 @@
             dma((nx,)), dma((nx,)),
             dma((nx,)), dma((nx,)),
             dma((ny,)), dma((ny,)),
-            dma((2,)),
+            dma((11,)),
         ],
         compiler_params=pltpu.CompilerParams(
-            collective_id=0, has_side_effects=True, vmem_limit_bytes=48 * 1024 * 1024
+            collective_id=0, has_side_effects=True, vmem_limit_bytes=67043328
         ),
     )(
         velocity.reshape(3, R * R, 128),

time: 68.9 us -> 61.2 us (0.89)
  local copies, waits for them, and re-layouts: 9.45 us -> 1.38 us
  Pallas kernels: 58.9 us -> 59.7 us
    unnamed x23 -> x1, local copies, waits for them, and re-layouts: 9.45 us -> 1.38 us
    pallas_call x1, Pallas kernels: 58.9 us -> 59.7 us  [on_device(): pl.pallas_call(functools.partial(kernel, sizes), out_shape=jax.ShapeDtype...]
where the time goes in v2:
time: 61.2 us; the launch traced here: 61 us
  Pallas kernels  59.7 us (98%)
  local copies, waits for them, and re-layouts  1.38 us (2%)
    pallas_call x1, Pallas kernels, on_device(): pl.pallas_call(functools.partial(kernel, sizes), out_shape=jax.ShapeDtype...  59.7 us
    unnamed x1, local copies, waits for them, and re-layouts  1.38 us

profile of v2, /device:TPU:1, one launch (start us, length us, event | category | flops | bytes accessed | tf_op | source)
XLA Modules:
  0.0 61.0 jit_solution(12469028179154899000)
XLA Ops:
  0.0 59.7 %shard_map.118 = f32[6,1024]{1,0:T(8,128)} custom-call(f32[3,256,128]{2,1,0:T(8,128)} %bitcast.5, s32[1,1024]{1,0:T(1,128)} %bitcast.6, s32[1,1024]{1,0:T(1,128)} %bitcast.7, s32[1,1024]{1,0:T(1,128)} %bitcast.8, s32[1,1024]{1,0:T(1,128)} %bitcast.9, f32[3,1024]{1,0:T(4,128)} %qw_hbm.1, bf16[16,144]{1,0:T(8,128)(2,1)} %constant.13.sub_hbm, ...), custom_call_target="tpu_custom_call" | custom-call | tf_op jit(solution)/shard_map/pallas_call | solution.py:462
  59.7 1.4 %copy.14 = f32[6,1024]{1,0:T(8,128)} copy(f32[6,1024]{1,0:T(8,128)} %shard_map.118) | data formatting | bytes 49152

commit v3 on v2

--- a/solution.py
+++ b/solution.py
@@ -347,7 +347,7 @@
             yb[f, pl.ds(pl.multiple_of(32 * n, 32) + R, R), :] = o[:, 128:]
             return 0
 
-        lax.fori_loop(0, R // 2, pair, 0)
+        lax.fori_loop(0, R // 2, pair, 0, unroll=True)
         for e in range(2):
             first = jnp.zeros((R, 128), F32)
             last = jnp.zeros((R, 128), F32)

time: 61.2 us -> 55.9 us (0.913)
  Pallas kernels: 59.7 us -> 54.4 us
    pallas_call x1, Pallas kernels: 59.7 us -> 54.4 us  [on_device(): pl.pallas_call(functools.partial(kernel, sizes), out_shape=jax.ShapeDtype...]
where the time goes in v3:
time: 55.9 us; the launch traced here: 55.8 us
  Pallas kernels  54.4 us (97%)
  local copies, waits for them, and re-layouts  1.38 us (2%)
    pallas_call x1, Pallas kernels, on_device(): pl.pallas_call(functools.partial(kernel, sizes), out_shape=jax.ShapeDtype...  54.4 us
    unnamed x1, local copies, waits for them, and re-layouts  1.38 us

profile of v3, /device:TPU:1, one launch (start us, length us, event | category | flops | bytes accessed | tf_op | source)
XLA Modules:
  0.0 55.8 jit_solution(5731653949872513194)
XLA Ops:
  0.0 54.4 %shard_map.118 = f32[6,1024]{1,0:T(8,128)} custom-call(f32[3,256,128]{2,1,0:T(8,128)} %bitcast.5, s32[1,1024]{1,0:T(1,128)} %bitcast.6, s32[1,1024]{1,0:T(1,128)} %bitcast.7, s32[1,1024]{1,0:T(1,128)} %bitcast.8, s32[1,1024]{1,0:T(1,128)} %bitcast.9, f32[3,1024]{1,0:T(4,128)} %qw_hbm.1, bf16[16,144]{1,0:T(8,128)(2,1)} %constant.13.sub_hbm, ...), custom_call_target="tpu_custom_call" | custom-call | tf_op jit(solution)/shard_map/pallas_call | solution.py:462
  54.4 1.4 %copy.14 = f32[6,1024]{1,0:T(8,128)} copy(f32[6,1024]{1,0:T(8,128)} %shard_map.118) | data formatting | bytes 49152

commit v4 on v3

--- a/solution.py
+++ b/solution.py
@@ -76,8 +76,8 @@
     v_ref, own_ref, cx_ref, cy_ref, cz_ref, qw_ref, sub_ref, mid_ref, midl_ref,
     u, xb, yb, zf, pack, halo, eh, el,
     sendq, gotq, passq, haveq, rows, w1h, w1l, wyb,
-    sth, stl, vals, sendr, gotr, passr, haver, onehot, rankhot,
-    s1, r1, s2, r2, s3, r3, sa, ra, sb, rb, sc, rc, sd, rd, lsem,
+    sth, stl, sendr, haver, onehot, rankhot,
+    s1, r1, s2, r2, s3, r3, sa, ra, sb, rb, sc, rc, lsem,
 ):
     nx, ny, nz = sizes
     g = [float(t) for t in taps()]
@@ -172,15 +172,18 @@
             remote(pack.at[1, f], halo.at[0, f], s3.at[f, 1], r3.at[f, 1], y_peer(1)),
         )
 
-    def exchange(n, peer_of, me, src, dst, ssem, rsem):
+    def exchange(n, peer_of, me, src, dst, place, ssem, rsem):
         copies = []
         for step in range(1, n):
             copies.append(
                 remote(
-                    src.at[lax.rem(me + step, n)], dst.at[me], ssem.at[step], rsem.at[step], peer_of(step)
+                    src.at[lax.rem(me + step, n)], dst.at[place[step]], ssem.at[step], rsem.at[step], peer_of(step)
                 )
             )
         return copies
+
+    far_y = [ny // 2 + m if h == 0 else ny // 2 - 1 - m for m in range(ny // 2) for h in range(2)]
+    place_y = [far_y.index(step) for step in range(ny)]
 
     for c in range(3):
         for copy in first_copies(c):
@@ -237,10 +240,10 @@
     for j in range(ny):
         sendq[j, 0] = head[j * nx : (j + 1) * nx]
         sendq[j, 1] = tail[j * nx : (j + 1) * nx]
-    out_y = exchange(ny, y_peer, my, sendq, gotq, sa, ra)
+    out_y = exchange(ny, y_peer, my, sendq, gotq, place_y, sa, ra)
     for copy in out_y:
         copy.start()
-    gotq[my] = sendq[my]
+    gotq[place_y[0]] = sendq[my]
 
     def first_filter(f):
         i, j = FIELDS[f]
@@ -267,10 +270,10 @@
         for i in range(nx):
             for k in range(2):
                 passq[i, k] = gotq[:, k, i, :]
-        out_x = exchange(nx, x_peer, mx, passq, haveq, sb, rb)
+        out_x = exchange(nx, x_peer, mx, passq, haveq, list(range(nx)), sb, rb)
         for copy in out_x:
             copy.start()
-        haveq[mx] = passq[mx]
+        haveq[0] = passq[mx]
         return out_x
 
     field = 0
@@ -286,21 +289,24 @@
     for copy in out_x:
         copy.wait_recv()
     half = owners // 2
-    table = [
-        jnp.concatenate([haveq[i, k] for i in range(nx)], axis=0) for k in range(2)
+    tops = [
+        jnp.concatenate([haveq[nx // 2 + i, k] for i in range(nx // 2)], axis=0) for k in range(2)
+    ]
+    bottoms = [
+        jnp.concatenate([haveq[nx // 2 - 1 - i, k] for i in range(nx // 2)], axis=0) for k in range(2)
     ]
     low = lane < CAP
 
-    def paired(x, second):
-        top, bottom = x[:half], x[half:]
+    def paired(k, second):
+        top, bottom = tops[k], bottoms[k]
         if second:
             return jnp.where(low, pltpu.roll(top, CAP, 1), bottom)
         return jnp.where(low, top, pltpu.roll(bottom, CAP, 1))
 
-    q_cell = paired(table[0], False).astype(jnp.int32)
-    q_wx = paired(table[0], True)
-    q_wy = paired(table[1], False)
-    q_wz = paired(table[1], True)
+    q_cell = paired(0, False).astype(jnp.int32)
+    q_wx = paired(0, True)
+    q_wy = paired(1, False)
+    q_wz = paired(1, True)
     q_cz = (q_cell >> 11).astype(F32)
     q_cx = ((q_cell >> 7) & (R - 1)).astype(F32)
     z_first = par == 0
@@ -388,46 +394,60 @@
         sth[128 * p : 128 * p + 128] = hi
         stl[128 * p : 128 * p + 128] = lo
 
+    me = my * nx + mx
+    per = ny // 2
+
+    def back(n, h, side):
+        step_x = nx // 2 + n // per if side == 0 else nx // 2 - 1 - n // per
+        step_y = ny // 2 + lax.rem(n, per) if h == 0 else ny // 2 - 1 - lax.rem(n, per)
+        holder = (lax.rem(mx + nx - step_x, nx), lax.rem(my + ny - step_y, ny), mz)
+        at = 2 * n + h
+        return remote(
+            sendr.at[at, side], haver.at[me], sc.at[at, side], rc.at[at, side], holder
+        )
+
+    def each_back(n, act):
+        for h in range(2):
+            for side in range(2):
+                if h == 1 and side == 1:
+
+                    @pl.when(n < chunks - 1)
+                    def _():
+                        act(back(n, 1, 1))
+
+                else:
+                    act(back(n, h, side))
+
     def interpolate(n, _):
         high = w1h[n]
         acc = dot(sth[...], high) + dot(stl[...], high) + dot(sth[...], w1l[n])
         wys = wyb[n]
-        for p in range(6):
-            v = jnp.sum(acc[128 * p : 128 * p + 128] * wys, axis=0, keepdims=True)
-            vals[p, pl.ds(2 * n, 1), :] = v[:, :128]
-            vals[p, pl.ds(2 * n + 1, 1), :] = v[:, 128:]
+        v = [
+            jnp.sum(acc[128 * p : 128 * p + 128] * wys, axis=0, keepdims=True) for p in range(6)
+        ]
+        for h in range(2):
+            for k in range(3):
+                a = v[2 * k][:, 128 * h : 128 * h + 128]
+                b = v[2 * k + 1][:, 128 * h : 128 * h + 128]
+                sendr[2 * n + h, 0, k : k + 1, :] = jnp.where(low, a, pltpu.roll(b, CAP, 1))
+                sendr[2 * n + h, 1, k : k + 1, :] = jnp.where(low, pltpu.roll(a, CAP, 1), b)
+        each_back(n, lambda copy: copy.start())
         return 0
 
     lax.fori_loop(0, chunks, interpolate, 0)
-
-    for k in range(3):
-        a, b = vals[2 * k], vals[2 * k + 1]
-        top = jnp.where(low, a, pltpu.roll(b, CAP, 1))
-        bottom = jnp.where(low, pltpu.roll(a, CAP, 1), b)
-        both = jnp.concatenate([top, bottom], axis=0)
-        for i in range(nx):
-            sendr[i, k] = both[i * ny : (i + 1) * ny]
-    back_x = exchange(nx, x_peer, mx, sendr, gotr, sc, rc)
-    for copy in back_x:
-        copy.start()
-    gotr[mx] = sendr[mx]
-    for copy in back_x:
-        copy.wait_recv()
-    for j in range(ny):
-        for k in range(3):
-            passr[j, k] = gotr[:, k, j, :]
-    back_y = exchange(ny, y_peer, my, passr, haver, sd, rd)
-    for copy in back_y:
-        copy.start()
-    haver[my] = passr[my]
-    for copy in back_y:
-        copy.wait_recv()
+    haver[me] = sendr[half - 1, 1]
+
+    def wait_back(n, _):
+        each_back(n, lambda copy: copy.wait_recv())
+        return 0
+
+    lax.fori_loop(0, chunks, wait_back, 0)
     pad = jnp.zeros((128 - owners, 128), F32)
     hot_pad = jnp.concatenate([onehot[...], jnp.zeros((128 - owners, count), BF16)], axis=0)
     hot_two = jnp.concatenate([hot_pad, hot_pad], axis=0)
     at_rank = rankhot[...]
     for k in range(3):
-        piece = jnp.concatenate([haver[j, k] for j in range(ny)] + [pad], axis=0)
+        piece = jnp.concatenate([haver[:, k, :], pad], axis=0)
         hi, lo = split(piece.T)
         picked = dot(jnp.concatenate([hi, lo], axis=1), hot_two)
         for h in range(2):
@@ -445,8 +465,14 @@
         return 0
 
     lax.fori_loop(0, 9, wait_sends, 0)
-    for copy in out_y + out_x + back_x + back_y:
+    for copy in out_y + out_x:
         copy.wait_send()
+
+    def wait_sent(n, _):
+        each_back(n, lambda copy: copy.wait_send())
+        return 0
+
+    lax.fori_loop(0, chunks, wait_sent, 0)
 
 
 def on_device(sizes, velocity, owner, cell_x, cell_y, cell_z, query_weights):
@@ -489,11 +515,8 @@
             pltpu.VMEM((chunks, 128, 256), F32),
             pltpu.VMEM((768, 256), BF16),
             pltpu.VMEM((768, 256), BF16),
-            pltpu.VMEM((6, half, 128), F32),
-            pltpu.VMEM((nx, 3, ny, 128), F32),
-            pltpu.VMEM((nx, 3, ny, 128), F32),
-            pltpu.VMEM((ny, 3, nx, 128), F32),
-            pltpu.VMEM((ny, 3, nx, 128), F32),
+            pltpu.VMEM((half, 2, 3, 128), F32),
+            pltpu.VMEM((owners, 3, 128), F32),
             pltpu.VMEM((owners, count), BF16),
             pltpu.VMEM((CAP, count), F32),
             dma((3, 2)), dma((3, 2)),
@@ -501,8 +524,7 @@
             dma((9, 2)), dma((9, 2)),
             dma((ny,)), dma((ny,)),
             dma((nx,)), dma((nx,)),
-            dma((nx,)), dma((nx,)),
-            dma((ny,)), dma((ny,)),
+            dma((half, 2)), dma((half, 2)),
             dma((11,)),
         ],
         compiler_params=pltpu.CompilerParams(

time: 55.9 us -> 52.6 us (0.941)
  Pallas kernels: 54.4 us -> 51 us
    pallas_call x1, Pallas kernels: 54.4 us -> 51 us  [on_device(): pl.pallas_call(functools.partial(kernel, sizes), out_shape=jax.ShapeDtype...]
where the time goes in v4:
time: 52.6 us; the launch traced here: 52.4 us
  Pallas kernels  51 us (97%)
  local copies, waits for them, and re-layouts  1.38 us (3%)
    pallas_call x1, Pallas kernels, on_device(): pl.pallas_call(functools.partial(kernel, sizes), out_shape=jax.ShapeDtype...  51 us
    unnamed x1, local copies, waits for them, and re-layouts  1.38 us

profile of v4, /device:TPU:1, one launch (start us, length us, event | category | flops | bytes accessed | tf_op | source)
XLA Modules:
  0.0 52.4 jit_solution(9107613507517641418)
XLA Ops:
  0.0 51.0 %shard_map.118 = f32[6,1024]{1,0:T(8,128)} custom-call(f32[3,256,128]{2,1,0:T(8,128)} %bitcast.5, s32[1,1024]{1,0:T(1,128)} %bitcast.6, s32[1,1024]{1,0:T(1,128)} %bitcast.7, s32[1,1024]{1,0:T(1,128)} %bitcast.8, s32[1,1024]{1,0:T(1,128)} %bitcast.9, f32[3,1024]{1,0:T(4,128)} %qw_hbm.1, bf16[16,144]{1,0:T(8,128)(2,1)} %constant.13.sub_hbm, ...), custom_call_target="tpu_custom_call" | custom-call | tf_op jit(solution)/shard_map/pallas_call | solution.py:488
  51.1 1.4 %copy.14 = f32[6,1024]{1,0:T(8,128)} copy(f32[6,1024]{1,0:T(8,128)} %shard_map.118) | data formatting | bytes 49152

commit v5 on v4

--- a/solution.py
+++ b/solution.py
@@ -16,6 +16,7 @@
 CAP = 64
 FIELDS = ((0, None), (0, 0), (1, None), (0, 1), (1, 1), (2, None), (0, 2), (1, 2), (2, 2))
 PAIRS = ((0, 0), (0, 1), (0, 2), (1, 1), (1, 2), (2, 2))
+DONE = ((0, 0), (0, 1), (1, 1), (0, 2), (1, 2), (2, 2))
 
 
 def taps():
@@ -47,12 +48,10 @@
     mid = band(by, by, R)
     left = band(R, by, 0)
     right = band(R, by, by + R)
-    groups = R // 2
-    edge = np.zeros((groups // 2, 2 * 128, 2 * by), np.float32)
-    for k in range(groups):
-        part = edge[k // 2, :, (k % 2) * by : (k % 2 + 1) * by]
-        part[R * k : R * k + R] = left
-        part[128 + R * k : 128 + R * k + R] = right
+    edge = np.zeros((256, 256), np.float32)
+    for k in range(R // 2):
+        edge[128 + R * k : 128 + R * k + R, 32 * k : 32 * k + R] = right[:, by - R :]
+        edge[R * k : R * k + R, 32 * k + R : 32 * k + 32] = left[:, :R]
     sh, sl = np_split(sub)
     mh, ml = np_split(mid)
     eh, el = np_split(edge)
@@ -75,8 +74,8 @@
     out_ref,
     v_ref, own_ref, cx_ref, cy_ref, cz_ref, qw_ref, sub_ref, mid_ref, midl_ref,
     u, xb, yb, zf, pack, halo, eh, el,
-    sendq, gotq, passq, haveq, rows, w1h, w1l, wyb,
-    sth, stl, sendr, haver, onehot, rankhot,
+    sendq, gotq, passq, haveq, rows, w1, wyb,
+    st, vals, sendr, haver, onehot, rankhot,
     s1, r1, s2, r2, s3, r3, sa, ra, sb, rb, sc, rc, lsem,
 ):
     nx, ny, nz = sizes
@@ -286,59 +285,68 @@
         if c == 0:
             out_x = pass_on()
 
-    for copy in out_x:
-        copy.wait_recv()
     half = owners // 2
-    tops = [
-        jnp.concatenate([haveq[nx // 2 + i, k] for i in range(nx // 2)], axis=0) for k in range(2)
-    ]
-    bottoms = [
-        jnp.concatenate([haveq[nx // 2 - 1 - i, k] for i in range(nx // 2)], axis=0) for k in range(2)
-    ]
     low = lane < CAP
-
-    def paired(k, second):
-        top, bottom = tops[k], bottoms[k]
-        if second:
-            return jnp.where(low, pltpu.roll(top, CAP, 1), bottom)
-        return jnp.where(low, top, pltpu.roll(bottom, CAP, 1))
-
-    q_cell = paired(0, False).astype(jnp.int32)
-    q_wx = paired(0, True)
-    q_wy = paired(1, False)
-    q_wz = paired(1, True)
-    q_cz = (q_cell >> 11).astype(F32)
-    q_cx = ((q_cell >> 7) & (R - 1)).astype(F32)
-    z_first = par == 0
-    rows[0] = jnp.where(z_first, q_cz, q_cx)
-    rows[1] = jnp.where(z_first, q_cx, q_cz)
-    rows[2] = (q_cell & 127).astype(F32)
-    rows[3] = jnp.where(z_first, q_wz, q_wx)
-    rows[4] = jnp.where(z_first, q_wx, q_wz)
-    rows[5] = q_wy
     chunks = owners * CAP // 256
 
-    def weights(n, _):
-        def row(k):
-            return jnp.concatenate([rows[k, pl.ds(2 * n, 1), :], rows[k, pl.ds(2 * n + 1, 1), :]], axis=1)
-
-        def hat(size, at, w):
-            index = lax.broadcasted_iota(jnp.int32, (size, 256), 0).astype(F32)
-            return jnp.where(index == at, 1.0 - w, jnp.where(index == at + 1.0, w, 0.0))
-
-        wa = hat(R, row(0), row(3))
-        wb = hat(R, row(1), row(4))
-        for a in range(R):
-            hi, lo = split(wa[a : a + 1] * wb)
-            w1h[n, R * a : R * a + R, :] = hi
-            w1l[n, R * a : R * a + R, :] = lo
-        wyb[n] = hat(128, row(2), row(5))
-        return 0
-
-    lax.fori_loop(0, chunks, weights, 0)
-
-    group = lax.broadcasted_iota(jnp.int32, (1, 128), 1) // R
-    for load in loads[6:9]:
+    def slot_weights():
+        for copy in out_x:
+            copy.wait_recv()
+        tops = [
+            jnp.concatenate([haveq[nx // 2 + i, k] for i in range(nx // 2)], axis=0) for k in range(2)
+        ]
+        bottoms = [
+            jnp.concatenate([haveq[nx // 2 - 1 - i, k] for i in range(nx // 2)], axis=0) for k in range(2)
+        ]
+
+        def paired(k, second):
+            top, bottom = tops[k], bottoms[k]
+            if second:
+                return jnp.where(low, pltpu.roll(top, CAP, 1), bottom)
+            return jnp.where(low, top, pltpu.roll(bottom, CAP, 1))
+
+        q_cell = paired(0, False).astype(jnp.int32)
+        q_wx = paired(0, True)
+        q_wy = paired(1, False)
+        q_wz = paired(1, True)
+        q_cz = (q_cell >> 11).astype(F32)
+        q_cx = ((q_cell >> 7) & (R - 1)).astype(F32)
+        z_first = par == 0
+        rows[0] = jnp.where(z_first, q_cz, q_cx)
+        rows[1] = jnp.where(z_first, q_cx, q_cz)
+        rows[2] = (q_cell & 127).astype(F32)
+        rows[3] = jnp.where(z_first, q_wz, q_wx)
+        rows[4] = jnp.where(z_first, q_wx, q_wz)
+        rows[5] = q_wy
+
+        def weights(n, _):
+            def row(k):
+                return jnp.concatenate([rows[k, pl.ds(2 * n, 1), :], rows[k, pl.ds(2 * n + 1, 1), :]], axis=1)
+
+            def index(size):
+                return lax.broadcasted_iota(jnp.int32, (size, 256), 0).astype(F32)
+
+            def eighth(x):
+                return jnp.floor(x * 256.0 + 0.5) * (1.0 / 256.0)
+
+            ca, cb, cy = row(0), row(1), row(2)
+            wa, wb, wy = eighth(row(3)), eighth(row(4)), row(5)
+            both = eighth(wa * wb)
+            ib = index(R)
+            lower, upper = ib == cb, ib == cb + 1.0
+            near = jnp.where(lower, 1.0 - wa - wb + both, jnp.where(upper, wb - both, 0.0))
+            far = jnp.where(lower, wa - both, jnp.where(upper, both, 0.0))
+            for a in range(R):
+                part = jnp.where(ca == float(a), near, jnp.where(ca == float(a - 1), far, 0.0))
+                w1[n, R * a : R * a + R, :] = part.astype(BF16)
+            iy = index(128)
+            wyb[n] = jnp.where(iy == cy, 1.0 - wy, jnp.where(iy == cy + 1.0, wy, 0.0))
+            return 0
+
+        lax.fori_loop(0, chunks, weights, 0)
+
+    group = lane // R
+    for load in loads[6:]:
         load.wait()
 
     def second_filter(f, _):
@@ -369,30 +377,59 @@
         zf[f] = dot(jnp.concatenate([hi, lo], axis=1), mid_ref[...]) + dot(hi, midl_ref[...])
         return 0
 
-    lax.fori_loop(0, 9, second_filter, 0)
-
-    for load in loads[9:]:
-        load.wait()
-
-    def wait_y(f, _):
-        for copy in y_copies(f):
-            copy.wait_recv()
-        return 0
-
-    lax.fori_loop(0, 9, wait_y, 0)
-    edges = jnp.concatenate([halo[0].reshape(9 * 32, 128), halo[1].reshape(9 * 32, 128)], axis=1)
-    eg_hi, eg_lo = split(edges)
-    for kk in range(R // 4):
-        part = dot(eg_hi, eh[kk]) + dot(eg_lo, eh[kk]) + dot(eg_hi, el[kk])
-        for k in range(2):
-            at = 32 * (2 * kk + k)
-            zf[:, at : at + 32, :] += part[:, 128 * k : 128 * k + 128].reshape(9, 32, 128)
-
-    for p, (i, j) in enumerate(PAIRS):
-        tau = zf[FIELDS.index((i, j))] - zf[FIELDS.index((i, None))] * zf[FIELDS.index((j, None))]
-        hi, lo = split(tau.T)
-        sth[128 * p : 128 * p + 128] = hi
-        stl[128 * p : 128 * p + 128] = lo
+    rim = (lane >= 128 - R) | (lane < R)
+
+    def finish(first, end):
+        def wait_y(f, _):
+            for copy in y_copies(f):
+                copy.wait_recv()
+            return 0
+
+        lax.fori_loop(first, end, wait_y, 0)
+        n = end - first
+        edges = jnp.concatenate(
+            [halo[side, first:end].reshape(32 * n, 128) for side in range(2)], axis=1
+        )
+        hi, lo = split(edges)
+        part = dot(hi, eh[...]) + dot(lo, eh[...]) + dot(hi, el[...])
+        for k in range(R // 2):
+            q, r = k // 4, k % 4
+            turned = pltpu.roll(part[:, 128 * q : 128 * q + 128], (128 - R - 32 * r) % 128, 1)
+            zf[first:end, 32 * k : 32 * k + 32, :] += jnp.where(rim, turned, 0.0).reshape(n, 32, 128)
+
+    def stress(first, end):
+        for d in range(first, end):
+            i, j = DONE[d]
+            tau = zf[FIELDS.index((i, j))] - zf[FIELDS.index((i, None))] * zf[FIELDS.index((j, None))]
+            hi, lo = split(tau.T)
+            st[d, :128] = hi
+            st[d, 128:] = lo
+
+    def at_queries(n, first, end):
+        acc = dot(st[first:end].reshape(256 * (end - first), 256), w1[n])
+        wys = wyb[n]
+        found = []
+        for d in range(end - first):
+            both = acc[256 * d : 256 * d + 128] + acc[256 * d + 128 : 256 * d + 256]
+            found.append(jnp.sum(both * wys, axis=0, keepdims=True))
+        return found
+
+    block = min(4, chunks)
+
+    def interpolate(first, end, number):
+        for n in range(block):
+            n = block * number + n
+            for d, v in enumerate(at_queries(n, first, end)):
+                p = PAIRS.index(DONE[first + d])
+                vals[p, pl.ds(2 * n, 1), :] = v[:, :128]
+                vals[p, pl.ds(2 * n + 1, 1), :] = v[:, 128:]
+
+    def interpolate_early(start, stop):
+        def step(number, _):
+            interpolate(0, 3, number)
+            return 0
+
+        lax.fori_loop(start, stop, step, 0)
 
     me = my * nx + mx
     per = ny // 2
@@ -418,23 +455,36 @@
                 else:
                     act(back(n, h, side))
 
-    def interpolate(n, _):
-        high = w1h[n]
-        acc = dot(sth[...], high) + dot(stl[...], high) + dot(sth[...], w1l[n])
-        wys = wyb[n]
-        v = [
-            jnp.sum(acc[128 * p : 128 * p + 128] * wys, axis=0, keepdims=True) for p in range(6)
-        ]
-        for h in range(2):
-            for k in range(3):
-                a = v[2 * k][:, 128 * h : 128 * h + 128]
-                b = v[2 * k + 1][:, 128 * h : 128 * h + 128]
-                sendr[2 * n + h, 0, k : k + 1, :] = jnp.where(low, a, pltpu.roll(b, CAP, 1))
-                sendr[2 * n + h, 1, k : k + 1, :] = jnp.where(low, pltpu.roll(a, CAP, 1), b)
-        each_back(n, lambda copy: copy.start())
+    def send_back(number, _):
+        interpolate(3, 6, number)
+
+        def send(n, _):
+            for h in range(2):
+                at = 2 * n + h
+                for k in range(3):
+                    a, b = vals[2 * k, pl.ds(at, 1), :], vals[2 * k + 1, pl.ds(at, 1), :]
+                    sendr[at, 0, k : k + 1, :] = jnp.where(low, a, pltpu.roll(b, CAP, 1))
+                    sendr[at, 1, k : k + 1, :] = jnp.where(low, pltpu.roll(a, CAP, 1), b)
+            each_back(n, lambda copy: copy.start())
+            return 0
+
+        lax.fori_loop(block * number, block * number + block, send, 0)
         return 0
 
-    lax.fori_loop(0, chunks, interpolate, 0)
+    def second_filters(first, end):
+        lax.fori_loop(first, end, second_filter, 0)
+
+    second_filters(0, 3)
+    slot_weights()
+    second_filters(3, 6)
+    finish(0, 5)
+    stress(0, 3)
+    interpolate_early(0, chunks // block // 2)
+    second_filters(6, 9)
+    interpolate_early(chunks // block // 2, chunks // block)
+    finish(5, 9)
+    stress(3, 6)
+    lax.fori_loop(0, chunks // block, send_back, 0)
     haver[me] = sendr[half - 1, 1]
 
     def wait_back(n, _):
@@ -503,18 +553,17 @@
             pltpu.VMEM((9, R * R, 128), F32),
             pltpu.VMEM((2, 9, 2, R, 128), F32),
             pltpu.VMEM((2, 9, 2, R, 128), F32),
-            pltpu.VMEM((4, 256, 256), BF16),
-            pltpu.VMEM((4, 256, 256), BF16),
+            pltpu.VMEM((256, 256), BF16),
+            pltpu.VMEM((256, 256), BF16),
             pltpu.VMEM((ny, 2, nx, 128), F32),
             pltpu.VMEM((ny, 2, nx, 128), F32),
             pltpu.VMEM((nx, 2, ny, 128), F32),
             pltpu.VMEM((nx, 2, ny, 128), F32),
             pltpu.VMEM((6, half, 128), F32),
             pltpu.VMEM((chunks, 256, 256), BF16),
-            pltpu.VMEM((chunks, 256, 256), BF16),
             pltpu.VMEM((chunks, 128, 256), F32),
-            pltpu.VMEM((768, 256), BF16),
-            pltpu.VMEM((768, 256), BF16),
+            pltpu.VMEM((6, 256, 256), BF16),
+            pltpu.VMEM((6, half, 128), F32),
             pltpu.VMEM((half, 2, 3, 128), F32),
             pltpu.VMEM((owners, 3, 128), F32),
             pltpu.VMEM((owners, count), BF16),

time: 52.6 us -> 48.9 us (0.930)
  Pallas kernels: 51 us -> 47.4 us
    pallas_call x1, Pallas kernels: 51 us -> 47.4 us  [on_device(): pl.pallas_call(functools.partial(kernel, sizes), out_shape=jax.ShapeDtype...]
where the time goes in v5:
time: 48.9 us; the launch traced here: 48.8 us
  Pallas kernels  47.4 us (97%)
  local copies, waits for them, and re-layouts  1.38 us (3%)
    pallas_call x1, Pallas kernels, on_device(): pl.pallas_call(functools.partial(kernel, sizes), out_shape=jax.ShapeDtype...  47.4 us
    unnamed x1, local copies, waits for them, and re-layouts  1.38 us

profile of v5, /device:TPU:1, one launch (start us, length us, event | category | flops | bytes accessed | tf_op | source)
XLA Modules:
  0.0 48.8 jit_solution(10933274097466152686)
XLA Ops:
  0.0 47.4 %shard_map.118 = f32[6,1024]{1,0:T(8,128)} custom-call(f32[3,256,128]{2,1,0:T(8,128)} %bitcast.5, s32[1,1024]{1,0:T(1,128)} %bitcast.6, s32[1,1024]{1,0:T(1,128)} %bitcast.7, s32[1,1024]{1,0:T(1,128)} %bitcast.8, s32[1,1024]{1,0:T(1,128)} %bitcast.9, f32[3,1024]{1,0:T(4,128)} %qw_hbm.1, bf16[16,144]{1,0:T(8,128)(2,1)} %constant.13.sub_hbm, ...), custom_call_target="tpu_custom_call" | custom-call | tf_op jit(solution)/shard_map/pallas_call | solution.py:538
  47.4 1.4 %copy.14 = f32[6,1024]{1,0:T(8,128)} copy(f32[6,1024]{1,0:T(8,128)} %shard_map.118) | data formatting | bytes 49152

commit v6 on v5

--- a/solution.py
+++ b/solution.py
@@ -76,7 +76,7 @@
     u, xb, yb, zf, pack, halo, eh, el,
     sendq, gotq, passq, haveq, rows, w1, wyb,
     st, vals, sendr, haver, onehot, rankhot,
-    s1, r1, s2, r2, s3, r3, sa, ra, sb, rb, sc, rc, lsem,
+    s1, r1, s2, r2, s3, r3, sa, ra, sb, rb, sc, rc, lsem, token,
 ):
     nx, ny, nz = sizes
     g = [float(t) for t in taps()]
@@ -109,7 +109,9 @@
         pltpu.make_async_copy(src, dst, lsem.at[number])
         for number, (src, dst) in enumerate(
             (
-                (v_hbm, v_ref),
+                (v_hbm.at[0], v_ref.at[0]),
+                (v_hbm.at[1], v_ref.at[1]),
+                (v_hbm.at[2], v_ref.at[2]),
                 (own_hbm, own_ref),
                 (cx_hbm, cx_ref),
                 (cy_hbm, cy_ref),
@@ -127,29 +129,18 @@
         load.start()
 
     barrier = pltpu.get_barrier_semaphore()
-    for step in range(1, nx):
-        pl.semaphore_signal(barrier, inc=1, device_id=x_peer(step), device_id_type=MESH)
-    for step in range(1, ny):
-        pl.semaphore_signal(barrier, inc=1, device_id=y_peer(step), device_id_type=MESH)
-    for step in (1, nz - 1):
-        pl.semaphore_signal(
-            barrier, inc=1, device_id=(mx, my, lax.rem(mz + step, nz)), device_id_type=MESH
-        )
-
-    loads[0].wait()
-
-    @pl.when(par == 0)
-    def _():
-        for c in range(3):
-            u[c, R : 2 * R] = v_ref[c].reshape(R, R, 128)
-
-    @pl.when(par == 1)
-    def _():
-        for c in range(3):
-            for b in range(R):
-                u[c, R + b] = v_ref[c, pl.ds(b, R, stride=R), :]
-
-    pl.semaphore_wait(barrier, nx - 1 + ny - 1 + 2)
+    near = (x_peer(1), x_peer(-1), y_peer(1), y_peer(-1))
+    for peer in near + ((mx, my, lax.rem(mz + 1, nz)), (mx, my, lax.rem(mz + nz - 1, nz))):
+        pl.semaphore_signal(barrier, inc=1, device_id=peer, device_id_type=MESH)
+
+    rounds = max(nx, ny) // 2 - 1
+
+    def tell(r):
+        for peer in near:
+            pl.semaphore_signal(token.at[r], inc=1, device_id=peer, device_id_type=MESH)
+
+    def hear(r):
+        pl.semaphore_wait(token.at[r], len(near))
 
     def first_copies(c):
         src = u.at[c, pl.ds(R, R)]
@@ -181,19 +172,33 @@
             )
         return copies
 
-    far_y = [ny // 2 + m if h == 0 else ny // 2 - 1 - m for m in range(ny // 2) for h in range(2)]
-    place_y = [far_y.index(step) for step in range(ny)]
+    far_x = [nx // 2 + m if h == 0 else nx // 2 - 1 - m for m in range(nx // 2) for h in range(2)]
+    place_x = [far_x.index(step) for step in range(nx)]
+    order_y = [ny // 2 + i for i in range(ny // 2)] + [ny // 2 - 1 - i for i in range(ny // 2)]
+    place_y = [order_y.index(step) for step in range(ny)]
 
     for c in range(3):
+        loads[c].wait()
+
+        @pl.when(par == 0)
+        def _():
+            u[c, R : 2 * R] = v_ref[c].reshape(R, R, 128)
+
+        @pl.when(par == 1)
+        def _():
+            for b in range(R):
+                u[c, R + b] = v_ref[c, pl.ds(b, R, stride=R), :]
+
+        if c == 0:
+            pl.semaphore_wait(barrier, len(near) + 2)
+            if rounds:
+                tell(0)
         for copy in first_copies(c):
             copy.start()
 
-    for load in loads[1:6]:
+    for load in loads[3:8]:
         load.wait()
-    bits_y = ny.bit_length() - 1
-    own = own_ref[...]
-    target = (own & (ny - 1)) * nx + (own >> bits_y)
-    hot = (lax.broadcasted_iota(jnp.int32, (owners, count), 0) == target).astype(F32)
+    hot = (lax.broadcasted_iota(jnp.int32, (owners, count), 0) == own_ref[...]).astype(F32)
     onehot[...] = hot.astype(BF16)
     earlier = (
         lax.broadcasted_iota(jnp.int32, (128, 128), 0) < lax.broadcasted_iota(jnp.int32, (128, 128), 1)
@@ -236,13 +241,15 @@
     scale = jnp.where(lane < CAP, 256.0, 1.0)
     head = spread[:, 0:128] * scale + spread[:, 128:256] + spread[:, 256:384]
     tail = spread[:, 384:512] + spread[:, 512:640] + spread[:, 640:768]
-    for j in range(ny):
-        sendq[j, 0] = head[j * nx : (j + 1) * nx]
-        sendq[j, 1] = tail[j * nx : (j + 1) * nx]
-    out_y = exchange(ny, y_peer, my, sendq, gotq, place_y, sa, ra)
-    for copy in out_y:
-        copy.start()
-    gotq[place_y[0]] = sendq[my]
+    for i in range(nx):
+        sendq[i, 0] = head[i * ny : (i + 1) * ny]
+        sendq[i, 1] = tail[i * ny : (i + 1) * ny]
+    out_x = exchange(nx, x_peer, mx, sendq, gotq, place_x, sa, ra)
+    gotq[place_x[0]] = sendq[mx]
+    if rounds:
+        hear(0)
+    if rounds > 1:
+        tell(1)
 
     def first_filter(f):
         i, j = FIELDS[f]
@@ -263,41 +270,47 @@
         for copy in second_copies(f):
             copy.start()
 
-    def pass_on():
-        for copy in out_y:
-            copy.wait_recv()
-        for i in range(nx):
-            for k in range(2):
-                passq[i, k] = gotq[:, k, i, :]
-        out_x = exchange(nx, x_peer, mx, passq, haveq, list(range(nx)), sb, rb)
-        for copy in out_x:
-            copy.start()
-        haveq[0] = passq[mx]
-        return out_x
-
     field = 0
     for c in range(3):
         for copy in first_copies(c):
             copy.wait_recv()
         for _ in range(c + 2):
+            if field == 0:
+                for r in range(1, rounds - 1):
+                    hear(r)
+                    tell(r + 1)
             first_filter(field)
+            if field == 0:
+                if rounds > 1:
+                    hear(rounds - 1)
+                for copy in out_x:
+                    copy.start()
             field += 1
-        if c == 0:
-            out_x = pass_on()
+
+    for copy in out_x:
+        copy.wait_recv()
+    for j in range(ny):
+        for k in range(2):
+            passq[j, k] = gotq[:, k, j, :]
+    out_y = exchange(ny, y_peer, my, passq, haveq, place_y, sb, rb)
+    for copy in out_y:
+        copy.start()
+    haveq[place_y[0]] = passq[my]
 
     half = owners // 2
     low = lane < CAP
     chunks = owners * CAP // 256
 
     def slot_weights():
-        for copy in out_x:
+        for copy in out_y:
             copy.wait_recv()
-        tops = [
-            jnp.concatenate([haveq[nx // 2 + i, k] for i in range(nx // 2)], axis=0) for k in range(2)
-        ]
-        bottoms = [
-            jnp.concatenate([haveq[nx // 2 - 1 - i, k] for i in range(nx // 2)], axis=0) for k in range(2)
-        ]
+        def table(k, start):
+            return jnp.concatenate(
+                [haveq[start : start + ny // 2, k, i, :] for i in range(nx)], axis=0
+            )
+
+        tops = [table(k, 0) for k in range(2)]
+        bottoms = [table(k, ny // 2) for k in range(2)]
 
         def paired(k, second):
             top, bottom = tops[k], bottoms[k]
@@ -346,7 +359,7 @@
         lax.fori_loop(0, chunks, weights, 0)
 
     group = lane // R
-    for load in loads[6:]:
+    for load in loads[8:]:
         load.wait()
 
     def second_filter(f, _):
@@ -431,14 +444,15 @@
 
         lax.fori_loop(start, stop, step, 0)
 
-    me = my * nx + mx
+    me = mx * ny + my
     per = ny // 2
 
     def back(n, h, side):
-        step_x = nx // 2 + n // per if side == 0 else nx // 2 - 1 - n // per
-        step_y = ny // 2 + lax.rem(n, per) if h == 0 else ny // 2 - 1 - lax.rem(n, per)
+        at = 2 * n + h
+        x, y = at // per, lax.rem(at, per)
+        step_x = nx // 2 + (1 - 2 * lax.rem(x, 2)) * ((x + 1) // 2)
+        step_y = ny // 2 + y if side == 0 else ny // 2 - 1 - y
         holder = (lax.rem(mx + nx - step_x, nx), lax.rem(my + ny - step_y, ny), mz)
-        at = 2 * n + h
         return remote(
             sendr.at[at, side], haver.at[me], sc.at[at, side], rc.at[at, side], holder
         )
@@ -474,9 +488,9 @@
     def second_filters(first, end):
         lax.fori_loop(first, end, second_filter, 0)
 
-    second_filters(0, 3)
+    second_filters(0, 5)
     slot_weights()
-    second_filters(3, 6)
+    second_filters(5, 6)
     finish(0, 5)
     stress(0, 3)
     interpolate_early(0, chunks // block // 2)
@@ -486,6 +500,25 @@
     stress(3, 6)
     lax.fori_loop(0, chunks // block, send_back, 0)
     haver[me] = sendr[half - 1, 1]
+
+    for c in range(3):
+        for copy in first_copies(c):
+            copy.wait_send()
+
+    def wait_sends(f, _):
+        for copy in second_copies(f) + y_copies(f):
+            copy.wait_send()
+        return 0
+
+    lax.fori_loop(0, 9, wait_sends, 0)
+    for copy in out_y + out_x:
+        copy.wait_send()
+
+    def wait_sent(n, _):
+        each_back(n, lambda copy: copy.wait_send())
+        return 0
+
+    lax.fori_loop(0, chunks, wait_sent, 0)
 
     def wait_back(n, _):
         each_back(n, lambda copy: copy.wait_recv())
@@ -504,25 +537,6 @@
             out_ref[2 * k + h : 2 * k + h + 1, :] = jnp.sum(
                 picked[CAP * h : CAP * h + CAP] * at_rank, axis=0, keepdims=True
             )
-
-    for c in range(3):
-        for copy in first_copies(c):
-            copy.wait_send()
-
-    def wait_sends(f, _):
-        for copy in second_copies(f) + y_copies(f):
-            copy.wait_send()
-        return 0
-
-    lax.fori_loop(0, 9, wait_sends, 0)
-    for copy in out_y + out_x:
-        copy.wait_send()
-
-    def wait_sent(n, _):
-        each_back(n, lambda copy: copy.wait_send())
-        return 0
-
-    lax.fori_loop(0, chunks, wait_sent, 0)
 
 
 def on_device(sizes, velocity, owner, cell_x, cell_y, cell_z, query_weights):
@@ -555,10 +569,10 @@
             pltpu.VMEM((2, 9, 2, R, 128), F32),
             pltpu.VMEM((256, 256), BF16),
             pltpu.VMEM((256, 256), BF16),
+            pltpu.VMEM((nx, 2, ny, 128), F32),
+            pltpu.VMEM((nx, 2, ny, 128), F32),
             pltpu.VMEM((ny, 2, nx, 128), F32),
             pltpu.VMEM((ny, 2, nx, 128), F32),
-            pltpu.VMEM((nx, 2, ny, 128), F32),
-            pltpu.VMEM((nx, 2, ny, 128), F32),
             pltpu.VMEM((6, half, 128), F32),
             pltpu.VMEM((chunks, 256, 256), BF16),
             pltpu.VMEM((chunks, 128, 256), F32),
@@ -571,22 +585,28 @@
             dma((3, 2)), dma((3, 2)),
             dma((9, 2)), dma((9, 2)),
             dma((9, 2)), dma((9, 2)),
+            dma((nx,)), dma((nx,)),
             dma((ny,)), dma((ny,)),
-            dma((nx,)), dma((nx,)),
             dma((half, 2)), dma((half, 2)),
-            dma((11,)),
+            dma((13,)),
+            pltpu.SemaphoreType.REGULAR((max(1, max(nx, ny) // 2 - 1),)),
         ],
         compiler_params=pltpu.CompilerParams(
-            collective_id=0, has_side_effects=True, vmem_limit_bytes=67043328
+            collective_id=0, has_side_effects=True, vmem_limit_bytes=40 * 1024 * 1024
         ),
     )(
-        velocity.reshape(3, R * R, 128),
-        owner.reshape(1, count),
-        cell_x.reshape(1, count),
-        cell_y.reshape(1, count),
-        cell_z.reshape(1, count),
-        query_weights,
-        *tables(velocity.shape[3]),
+        *[
+            pltpu.with_memory_space_constraint(x, pltpu.HBM)
+            for x in (
+                velocity.reshape(3, R * R, 128),
+                owner.reshape(1, count),
+                cell_x.reshape(1, count),
+                cell_y.reshape(1, count),
+                cell_z.reshape(1, count),
+                query_weights,
+                *tables(velocity.shape[3]),
+            )
+        ]
     )
 
 

time: 48.9 us -> 46.2 us (0.945)
  Pallas kernels: 47.4 us -> 45.5 us
  local copies, waits for them, and re-layouts: 1.38 us -> 0.62 us
    pallas_call x1, Pallas kernels: 47.4 us -> 45.5 us  [on_device(): pl.pallas_call(functools.partial(kernel, sizes), out_shape=jax.ShapeDtype...]
    unnamed x1, local copies, waits for them, and re-layouts: 1.38 us -> 0.62 us
where the time goes in v6:
time: 46.2 us; the launch traced here: 46.1 us
  Pallas kernels  45.5 us (98%)
  local copies, waits for them, and re-layouts  0.62 us (1%)
    pallas_call x1, Pallas kernels, on_device(): pl.pallas_call(functools.partial(kernel, sizes), out_shape=jax.ShapeDtype...  45.5 us

profile of v6, /device:TPU:1, one launch (start us, length us, event | category | flops | bytes accessed | tf_op | source)
XLA Modules:
  0.0 46.1 jit_solution(4260591086659520651)
XLA Ops:
  0.0 45.5 %shard_map.118 = f32[6,1024]{1,0:T(8,128)S(1)} custom-call(f32[3,256,128]{2,1,0:T(8,128)} %bitcast.5, s32[1,1024]{1,0:T(1,128)} %bitcast.6, s32[1,1024]{1,0:T(1,128)} %bitcast.7, s32[1,1024]{1,0:T(1,128)} %bitcast.8, s32[1,1024]{1,0:T(1,128)} %bitcast.9, f32[3,1024]{1,0:T(4,128)} %qw_hbm.1, bf16[16,144]{1,0:T(8,128)(2,1)} %constant.13.sub_hbm, ...), custom_call_target="tpu_custom_call" | custom-call | tf_op jit(solution)/shard_map/pallas_call | solution.py:552
  45.5 0.6 %copy.14 = f32[6,1024]{1,0:T(8,128)} copy(f32[6,1024]{1,0:T(8,128)S(1)} %shard_map.118) | data formatting | bytes 49152

commit v7 on v6

--- a/solution.py
+++ b/solution.py
@@ -429,13 +429,23 @@
 
     block = min(4, chunks)
 
+    def pack_row(at, k, a, b):
+        sendr[at, 0, k : k + 1, :] = jnp.where(low, a, pltpu.roll(b, CAP, 1))
+        sendr[at, 1, k : k + 1, :] = jnp.where(low, pltpu.roll(a, CAP, 1), b)
+
     def interpolate(first, end, number):
         for n in range(block):
             n = block * number + n
-            for d, v in enumerate(at_queries(n, first, end)):
-                p = PAIRS.index(DONE[first + d])
-                vals[p, pl.ds(2 * n, 1), :] = v[:, :128]
-                vals[p, pl.ds(2 * n + 1, 1), :] = v[:, 128:]
+            found = at_queries(n, first, end)
+            for h in range(2):
+                at = 2 * n + h
+                v = [w[:, 128 * h : 128 * h + 128] for w in found]
+                if first == 0:
+                    pack_row(at, 0, v[0], v[1])
+                    vals[pl.ds(at, 1), :] = v[2]
+                else:
+                    pack_row(at, 1, vals[pl.ds(at, 1), :], v[0])
+                    pack_row(at, 2, v[1], v[2])
 
     def interpolate_early(start, stop):
         def step(number, _):
@@ -473,12 +483,6 @@
         interpolate(3, 6, number)
 
         def send(n, _):
-            for h in range(2):
-                at = 2 * n + h
-                for k in range(3):
-                    a, b = vals[2 * k, pl.ds(at, 1), :], vals[2 * k + 1, pl.ds(at, 1), :]
-                    sendr[at, 0, k : k + 1, :] = jnp.where(low, a, pltpu.roll(b, CAP, 1))
-                    sendr[at, 1, k : k + 1, :] = jnp.where(low, pltpu.roll(a, CAP, 1), b)
             each_back(n, lambda copy: copy.start())
             return 0
 
@@ -488,14 +492,12 @@
     def second_filters(first, end):
         lax.fori_loop(first, end, second_filter, 0)
 
-    second_filters(0, 5)
+    second_filters(0, 6)
     slot_weights()
-    second_filters(5, 6)
     finish(0, 5)
     stress(0, 3)
-    interpolate_early(0, chunks // block // 2)
     second_filters(6, 9)
-    interpolate_early(chunks // block // 2, chunks // block)
+    interpolate_early(0, chunks // block)
     finish(5, 9)
     stress(3, 6)
     lax.fori_loop(0, chunks // block, send_back, 0)
@@ -525,16 +527,16 @@
         return 0
 
     lax.fori_loop(0, chunks, wait_back, 0)
-    pad = jnp.zeros((128 - owners, 128), F32)
-    hot_pad = jnp.concatenate([onehot[...], jnp.zeros((128 - owners, count), BF16)], axis=0)
-    hot_two = jnp.concatenate([hot_pad, hot_pad], axis=0)
+    hot_two = jnp.concatenate([onehot[...], onehot[...]], axis=0)
     at_rank = rankhot[...]
     for k in range(3):
-        piece = jnp.concatenate([haver[:, k, :], pad], axis=0)
-        hi, lo = split(piece.T)
-        picked = dot(jnp.concatenate([hi, lo], axis=1), hot_two)
+        piece = haver[:, k, :]
+        hi = piece.astype(BF16).astype(F32)
+        both = jnp.concatenate([hi, piece - hi], axis=0).T.astype(BF16)
+        picked = dot(both, hot_two)
         for h in range(2):
-            out_ref[2 * k + h : 2 * k + h + 1, :] = jnp.sum(
+            p = PAIRS.index(DONE[2 * k + h])
+            out_ref[p : p + 1, :] = jnp.sum(
                 picked[CAP * h : CAP * h + CAP] * at_rank, axis=0, keepdims=True
             )
 
@@ -577,7 +579,7 @@
             pltpu.VMEM((chunks, 256, 256), BF16),
             pltpu.VMEM((chunks, 128, 256), F32),
             pltpu.VMEM((6, 256, 256), BF16),
-            pltpu.VMEM((6, half, 128), F32),
+            pltpu.VMEM((half, 128), F32),
             pltpu.VMEM((half, 2, 3, 128), F32),
             pltpu.VMEM((owners, 3, 128), F32),
             pltpu.VMEM((owners, count), BF16),

time: 46.2 us -> 46 us (level)
  no operation moved by 1% of the time
where the time goes in v7:
time: 46 us; the launch traced here: 45.9 us
  Pallas kernels  45.3 us (98%)
  local copies, waits for them, and re-layouts  0.62 us (1%)
    pallas_call x1, Pallas kernels, on_device(): pl.pallas_call(functools.partial(kernel, sizes), out_shape=jax.ShapeDtype...  45.3 us

profile of v7, /device:TPU:1, one launch (start us, length us, event | category | flops | bytes accessed | tf_op | source)
XLA Modules:
  0.0 45.9 jit_solution(17500949968233274184)
XLA Ops:
  0.0 45.3 %shard_map.118 = f32[6,1024]{1,0:T(8,128)S(1)} custom-call(f32[3,256,128]{2,1,0:T(8,128)} %bitcast.5, s32[1,1024]{1,0:T(1,128)} %bitcast.6, s32[1,1024]{1,0:T(1,128)} %bitcast.7, s32[1,1024]{1,0:T(1,128)} %bitcast.8, s32[1,1024]{1,0:T(1,128)} %bitcast.9, f32[3,1024]{1,0:T(4,128)} %qw_hbm.1, bf16[16,144]{1,0:T(8,128)(2,1)} %constant.13.sub_hbm, ...), custom_call_target="tpu_custom_call" | custom-call | tf_op jit(solution)/shard_map/pallas_call | solution.py:554
  45.3 0.6 %copy.14 = f32[6,1024]{1,0:T(8,128)} copy(f32[6,1024]{1,0:T(8,128)S(1)} %shard_map.118) | data formatting | bytes 49152

commit v8 on v7

--- a/solution.py
+++ b/solution.py
@@ -76,7 +76,7 @@
     u, xb, yb, zf, pack, halo, eh, el,
     sendq, gotq, passq, haveq, rows, w1, wyb,
     st, vals, sendr, haver, onehot, rankhot,
-    s1, r1, s2, r2, s3, r3, sa, ra, sb, rb, sc, rc, lsem, token,
+    s1, r1, s2, r2, s3, r3, sa, ra, sb, rb, sc, rc, lsem, token, clear,
 ):
     nx, ny, nz = sizes
     g = [float(t) for t in taps()]
@@ -95,7 +95,7 @@
         )
 
     def y_peer(step):
-        return (mx, lax.rem(my + step % ny, ny), mz)
+        return (mx, lax.rem(my + ny + step, ny), mz)
 
     def x_peer(step):
         return (lax.rem(mx + step % nx, nx), my, mz)
@@ -251,6 +251,10 @@
     if rounds > 1:
         tell(1)
 
+    for copy in first_copies(0):
+        copy.wait_send()
+    pl.semaphore_signal(clear, inc=1, device_id=y_peer(1 - 2 * par), device_id_type=MESH)
+
     def first_filter(f):
         i, j = FIELDS[f]
 
@@ -279,8 +283,9 @@
                 for r in range(1, rounds - 1):
                     hear(r)
                     tell(r + 1)
+                pl.semaphore_wait(clear, 1)
             first_filter(field)
-            if field == 0:
+            if field == 1:
                 if rounds > 1:
                     hear(rounds - 1)
                 for copy in out_x:
@@ -296,6 +301,26 @@
     for copy in out_y:
         copy.start()
     haveq[place_y[0]] = passq[my]
+
+    def hops(chunk):
+        step = far_x[2 * chunk // (ny // 2)]
+        return min(step, nx - step) + min(2, ny // 4) - 2 * chunk % (ny // 2) // 2
+
+    order = sorted(range(owners * CAP // 256), key=lambda chunk: -hops(chunk))
+    codes = [
+        int(np.uint32(sum(c << (4 * i) for i, c in enumerate(order[at : at + 8]))).astype(np.int32))
+        for at in range(0, len(order), 8)
+    ]
+
+    def natural(n):
+        code = codes[0] if len(codes) == 1 else jnp.where(n < 8, codes[0], codes[1])
+        return lax.shift_right_logical(jnp.int32(code), 4 * (n & 7)) & 15
+
+    def quotient(a, b):
+        return a >> (b.bit_length() - 1) if b & (b - 1) == 0 else lax.div(a, b)
+
+    def remainder(a, b):
+        return a & (b - 1) if b & (b - 1) == 0 else lax.rem(a, b)
 
     half = owners // 2
     low = lane < CAP
@@ -333,8 +358,10 @@
         rows[5] = q_wy
 
         def weights(n, _):
+            at = natural(n)
+
             def row(k):
-                return jnp.concatenate([rows[k, pl.ds(2 * n, 1), :], rows[k, pl.ds(2 * n + 1, 1), :]], axis=1)
+                return jnp.concatenate([rows[k, pl.ds(2 * at, 1), :], rows[k, pl.ds(2 * at + 1, 1), :]], axis=1)
 
             def index(size):
                 return lax.broadcasted_iota(jnp.int32, (size, 256), 0).astype(F32)
@@ -459,10 +486,11 @@
 
     def back(n, h, side):
         at = 2 * n + h
-        x, y = at // per, lax.rem(at, per)
-        step_x = nx // 2 + (1 - 2 * lax.rem(x, 2)) * ((x + 1) // 2)
+        where = 2 * natural(n) + h
+        x, y = quotient(where, per), remainder(where, per)
+        step_x = nx // 2 + (1 - 2 * (x & 1)) * ((x + 1) >> 1)
         step_y = ny // 2 + y if side == 0 else ny // 2 - 1 - y
-        holder = (lax.rem(mx + nx - step_x, nx), lax.rem(my + ny - step_y, ny), mz)
+        holder = (remainder(mx + nx - step_x, nx), remainder(my + ny - step_y, ny), mz)
         return remote(
             sendr.at[at, side], haver.at[me], sc.at[at, side], rc.at[at, side], holder
         )
@@ -503,7 +531,7 @@
     lax.fori_loop(0, chunks // block, send_back, 0)
     haver[me] = sendr[half - 1, 1]
 
-    for c in range(3):
+    for c in range(1, 3):
         for copy in first_copies(c):
             copy.wait_send()
 
@@ -592,6 +620,7 @@
             dma((half, 2)), dma((half, 2)),
             dma((13,)),
             pltpu.SemaphoreType.REGULAR((max(1, max(nx, ny) // 2 - 1),)),
+            pltpu.SemaphoreType.REGULAR,
         ],
         compiler_params=pltpu.CompilerParams(
             collective_id=0, has_side_effects=True, vmem_limit_bytes=40 * 1024 * 1024

time: 46 us -> 45.1 us (0.980)
  Pallas kernels: 45.3 us -> 44.4 us
    pallas_call x1, Pallas kernels: 45.3 us -> 44.4 us  [on_device(): pl.pallas_call(functools.partial(kernel, sizes), out_shape=jax.ShapeDtype...]
where the time goes in v8:
time: 45.1 us; the launch traced here: 45 us
  Pallas kernels  44.4 us (98%)
  local copies, waits for them, and re-layouts  0.62 us (1%)
    pallas_call x1, Pallas kernels, on_device(): pl.pallas_call(functools.partial(kernel, sizes), out_shape=jax.ShapeDtype...  44.4 us

profile of v8, /device:TPU:1, one launch (start us, length us, event | category | flops | bytes accessed | tf_op | source)
XLA Modules:
  0.0 45.0 jit_solution(9677360333017002838)
XLA Ops:
  0.0 44.4 %shard_map.118 = f32[6,1024]{1,0:T(8,128)S(1)} custom-call(f32[3,256,128]{2,1,0:T(8,128)} %bitcast.5, s32[1,1024]{1,0:T(1,128)} %bitcast.6, s32[1,1024]{1,0:T(1,128)} %bitcast.7, s32[1,1024]{1,0:T(1,128)} %bitcast.8, s32[1,1024]{1,0:T(1,128)} %bitcast.9, f32[3,1024]{1,0:T(4,128)} %qw_hbm.1, bf16[16,144]{1,0:T(8,128)(2,1)} %constant.13.sub_hbm, ...), custom_call_target="tpu_custom_call" | custom-call | tf_op jit(solution)/shard_map/pallas_call | solution.py:582
  44.4 0.6 %copy.14 = f32[6,1024]{1,0:T(8,128)} copy(f32[6,1024]{1,0:T(8,128)S(1)} %shard_map.118) | data formatting | bytes 49152

commit v9 on v8

--- a/solution.py
+++ b/solution.py
@@ -517,6 +517,8 @@
         lax.fori_loop(block * number, block * number + block, send, 0)
         return 0
 
+    early = 1 if chunks // block > 1 else 0
+
     def second_filters(first, end):
         lax.fori_loop(first, end, second_filter, 0)
 
@@ -524,8 +526,10 @@
     slot_weights()
     finish(0, 5)
     stress(0, 3)
-    second_filters(6, 9)
-    interpolate_early(0, chunks // block)
+    second_filters(6, 8)
+    interpolate_early(0, early)
+    second_filters(8, 9)
+    interpolate_early(early, chunks // block)
     finish(5, 9)
     stress(3, 6)
     lax.fori_loop(0, chunks // block, send_back, 0)

time: 45.1 us -> 44.6 us (0.989)
  Pallas kernels: 44.4 us -> 43.9 us
    pallas_call x1, Pallas kernels: 44.4 us -> 43.9 us  [on_device(): pl.pallas_call(functools.partial(kernel, sizes), out_shape=jax.ShapeDtype...]
where the time goes in v9:
time: 44.6 us; the launch traced here: 44.5 us
  Pallas kernels  43.9 us (98%)
  local copies, waits for them, and re-layouts  0.62 us (1%)
    pallas_call x1, Pallas kernels, on_device(): pl.pallas_call(functools.partial(kernel, sizes), out_shape=jax.ShapeDtype...  43.9 us

profile of v9, /device:TPU:1, one launch (start us, length us, event | category | flops | bytes accessed | tf_op | source)
XLA Modules:
  0.0 44.5 jit_solution(15687998581874024856)
XLA Ops:
  0.0 43.9 %shard_map.118 = f32[6,1024]{1,0:T(8,128)S(1)} custom-call(f32[3,256,128]{2,1,0:T(8,128)} %bitcast.5, s32[1,1024]{1,0:T(1,128)} %bitcast.6, s32[1,1024]{1,0:T(1,128)} %bitcast.7, s32[1,1024]{1,0:T(1,128)} %bitcast.8, s32[1,1024]{1,0:T(1,128)} %bitcast.9, f32[3,1024]{1,0:T(4,128)} %qw_hbm.1, bf16[16,144]{1,0:T(8,128)(2,1)} %constant.13.sub_hbm, ...), custom_call_target="tpu_custom_call" | custom-call | tf_op jit(solution)/shard_map/pallas_call | solution.py:586
  43.9 0.6 %copy.14 = f32[6,1024]{1,0:T(8,128)} copy(f32[6,1024]{1,0:T(8,128)S(1)} %shard_map.118) | data formatting | bytes 49152

commit v10 on v9

--- a/solution.py
+++ b/solution.py
@@ -460,9 +460,9 @@
         sendr[at, 0, k : k + 1, :] = jnp.where(low, a, pltpu.roll(b, CAP, 1))
         sendr[at, 1, k : k + 1, :] = jnp.where(low, pltpu.roll(a, CAP, 1), b)
 
-    def interpolate(first, end, number):
-        for n in range(block):
-            n = block * number + n
+    def interpolate(first, end, start, size):
+        for n in range(size):
+            n = start + n
             found = at_queries(n, first, end)
             for h in range(2):
                 at = 2 * n + h
@@ -476,7 +476,7 @@
 
     def interpolate_early(start, stop):
         def step(number, _):
-            interpolate(0, 3, number)
+            interpolate(0, 3, block * number, block)
             return 0
 
         lax.fori_loop(start, stop, step, 0)
@@ -508,7 +508,7 @@
                     act(back(n, h, side))
 
     def send_back(number, _):
-        interpolate(3, 6, number)
+        interpolate(3, 6, block * number, block)
 
         def send(n, _):
             each_back(n, lambda copy: copy.start())
@@ -529,9 +529,15 @@
     second_filters(6, 8)
     interpolate_early(0, early)
     second_filters(8, 9)
-    interpolate_early(early, chunks // block)
-    finish(5, 9)
-    stress(3, 6)
+    if chunks % 8 == 0:
+        interpolate(0, 3, block, 6)
+        interpolate(0, 3, block + 6, chunks - block - 6)
+    else:
+        interpolate_early(early, chunks // block)
+    finish(5, 8)
+    stress(3, 5)
+    finish(8, 9)
+    stress(5, 6)
     lax.fori_loop(0, chunks // block, send_back, 0)
     haver[me] = sendr[half - 1, 1]
 

time: 44.6 us -> 44.4 us (level)
  no operation moved by 1% of the time
where the time goes in v10:
time: 44.4 us; the launch traced here: 44.3 us
  Pallas kernels  43.7 us (98%)
  local copies, waits for them, and re-layouts  0.62 us (1%)
    pallas_call x1, Pallas kernels, on_device(): pl.pallas_call(functools.partial(kernel, sizes), out_shape=jax.ShapeDtype...  43.7 us

profile of v10, /device:TPU:1, one launch (start us, length us, event | category | flops | bytes accessed | tf_op | source)
XLA Modules:
  0.0 44.3 jit_solution(14158627422741209484)
XLA Ops:
  0.0 43.7 %shard_map.118 = f32[6,1024]{1,0:T(8,128)S(1)} custom-call(f32[3,256,128]{2,1,0:T(8,128)} %bitcast.5, s32[1,1024]{1,0:T(1,128)} %bitcast.6, s32[1,1024]{1,0:T(1,128)} %bitcast.7, s32[1,1024]{1,0:T(1,128)} %bitcast.8, s32[1,1024]{1,0:T(1,128)} %bitcast.9, f32[3,1024]{1,0:T(4,128)} %qw_hbm.1, bf16[16,144]{1,0:T(8,128)(2,1)} %constant.13.sub_hbm, ...), custom_call_target="tpu_custom_call" | custom-call | tf_op jit(solution)/shard_map/pallas_call | solution.py:592
  43.7 0.6 %copy.14 = f32[6,1024]{1,0:T(8,128)} copy(f32[6,1024]{1,0:T(8,128)S(1)} %shard_map.118) | data formatting | bytes 49152

commit v11 on v10

--- a/solution.py
+++ b/solution.py
@@ -285,7 +285,7 @@
                     tell(r + 1)
                 pl.semaphore_wait(clear, 1)
             first_filter(field)
-            if field == 1:
+            if field == 0:
                 if rounds > 1:
                     hear(rounds - 1)
                 for copy in out_x:

time: 44.4 us -> 44.4 us (level)
  no operation moved by 1% of the time
where the time goes in v11:
time: 44.4 us; the launch traced here: 44.3 us
  Pallas kernels  43.7 us (98%)
  local copies, waits for them, and re-layouts  0.62 us (1%)
    pallas_call x1, Pallas kernels, on_device(): pl.pallas_call(functools.partial(kernel, sizes), out_shape=jax.ShapeDtype...  43.7 us

profile of v11, /device:TPU:1, one launch (start us, length us, event | category | flops | bytes accessed | tf_op | source)
XLA Modules:
  0.0 44.3 jit_solution(15951807023325000817)
XLA Ops:
  0.0 43.7 %shard_map.118 = f32[6,1024]{1,0:T(8,128)S(1)} custom-call(f32[3,256,128]{2,1,0:T(8,128)} %bitcast.5, s32[1,1024]{1,0:T(1,128)} %bitcast.6, s32[1,1024]{1,0:T(1,128)} %bitcast.7, s32[1,1024]{1,0:T(1,128)} %bitcast.8, s32[1,1024]{1,0:T(1,128)} %bitcast.9, f32[3,1024]{1,0:T(4,128)} %qw_hbm.1, bf16[16,144]{1,0:T(8,128)(2,1)} %constant.13.sub_hbm, ...), custom_call_target="tpu_custom_call" | custom-call | tf_op jit(solution)/shard_map/pallas_call | solution.py:592
  43.7 0.6 %copy.14 = f32[6,1024]{1,0:T(8,128)} copy(f32[6,1024]{1,0:T(8,128)S(1)} %shard_map.118) | data formatting | bytes 49152

commit v12 on v10

--- a/solution.py
+++ b/solution.py
@@ -530,8 +530,7 @@
     interpolate_early(0, early)
     second_filters(8, 9)
     if chunks % 8 == 0:
-        interpolate(0, 3, block, 6)
-        interpolate(0, 3, block + 6, chunks - block - 6)
+        interpolate(0, 3, block, chunks - block)
     else:
         interpolate_early(early, chunks // block)
     finish(5, 8)

time: 44.4 us -> 44.4 us (level)
  no operation moved by 1% of the time
where the time goes in v12:
time: 44.4 us; the launch traced here: 44.3 us
  Pallas kernels  43.7 us (98%)
  local copies, waits for them, and re-layouts  0.62 us (1%)
    pallas_call x1, Pallas kernels, on_device(): pl.pallas_call(functools.partial(kernel, sizes), out_shape=jax.ShapeDtype...  43.7 us

profile of v12, /device:TPU:1, one launch (start us, length us, event | category | flops | bytes accessed | tf_op | source)
XLA Modules:
  0.0 44.3 jit_solution(14158627422741209484)
XLA Ops:
  0.0 43.7 %shard_map.118 = f32[6,1024]{1,0:T(8,128)S(1)} custom-call(f32[3,256,128]{2,1,0:T(8,128)} %bitcast.5, s32[1,1024]{1,0:T(1,128)} %bitcast.6, s32[1,1024]{1,0:T(1,128)} %bitcast.7, s32[1,1024]{1,0:T(1,128)} %bitcast.8, s32[1,1024]{1,0:T(1,128)} %bitcast.9, f32[3,1024]{1,0:T(4,128)} %qw_hbm.1, bf16[16,144]{1,0:T(8,128)(2,1)} %constant.13.sub_hbm, ...), custom_call_target="tpu_custom_call" | custom-call | tf_op jit(solution)/shard_map/pallas_call | solution.py:591
  43.7 0.6 %copy.14 = f32[6,1024]{1,0:T(8,128)} copy(f32[6,1024]{1,0:T(8,128)S(1)} %shard_map.118) | data formatting | bytes 49152
